TPU v7x, 256 devices: a whole 4x4x8 slice. The times are simulated.
256 devices in a mesh: dp: 64 (over x, y, z_lo, core), tensor: 4 (over z_hi).
Axes of the slice: x: 4, y: 4, z: 8 (z_hi: 4, z_lo: 2; z = z_hi * 2 + z_lo), core: 2. Of those that a mesh axis runs over, the one named last changes fastest.
Arguments:
- activations: bfloat16 [49152, 8192], P('dp'), may hold values from -48 to 48
- cotangent: bfloat16 [49152, 1024], P('dp', 'tensor'), may hold values from -0.375 to 0.375
- sampled_rows: int32 [4096], P('dp'), may hold values from 0 to 767
- block_owner: int32 [32], replicated, may hold values from 0 to 63, as said below
Outputs:
- natural_step: float32 [8192, 1024], P('dp', 'tensor')
- owner_block_inverses: float32 [64, 256, 256], P('dp')
Inputs may be any that keep to these rules, and one draw needn't show every extreme that they name: `block_owner`: each index of dp owns either no block or exactly 1 block; block 0 is owned by index 32.
All inputs are finite; a program needn't handle non-finite values. Where the computation divides by a largest or mean magnitude, that divisor is 1e-20 or more.
Results may differ from a plain program's by a relative error of at most 0.0003.
Values may be sent and summed in bfloat16 or wider, within the bound.
A program may use at most 128 MiB of HBM per device.

v0:
```python
import jax
import jax.numpy as jnp
from jax import lax
from jax.sharding import PartitionSpec as P

S_DEV = 64
FACTOR_BLOCK = 256
ITERS = 10


DAMPING = 0.05
precise_mode = lax.Precision.HIGHEST


def from_partner(block, axis, apart):
    count = lax.axis_size(axis)
    route = []
    for low in range(count):
        high = low | 1 << apart
        if high != low and high < count:
            route += [(low, high), (high, low)]
    return lax.ppermute(block, axis, route)


def newton_inverse(matrix):
    extent = matrix.shape[-1]
    identity = jnp.eye(extent, dtype=jnp.float32)
    row_bound = jnp.max(jnp.sum(jnp.abs(matrix), axis=2), axis=1)
    initial = identity[None, :, :] / row_bound[:, None, None]

    def advance(turn_index, current):
        product = jnp.einsum("nij,njk->nik", matrix, current, precision=precise_mode)
        return jnp.einsum(
            "nij,njk->nik", current, 2.0 * identity[None, :, :] - product, precision=precise_mode
        )

    return lax.fori_loop(0, ITERS, advance, initial)


def block_rank(block_owner):
    block_total = block_owner.shape[0]
    same_owner = block_owner[:, None] == block_owner[None, :]
    positions = jnp.arange(block_total, dtype=jnp.int32)
    before = positions[None, :] < positions[:, None]
    return jnp.sum((same_owner & before).astype(jnp.int32), axis=1)


def owner_grams(received):
    return jnp.einsum("pcsk,pcsl->ckl", received, received, preferred_element_type=jnp.float32)


def per_device(activations, cotangent, sampled_rows, block_owner):
    tok_local = activations.shape[0]
    model_width = activations.shape[1]
    group_w = cotangent.shape[1]
    dp_count = lax.axis_size("dp")
    my_dp = lax.axis_index("dp")
    block_total = model_width // FACTOR_BLOCK
    capacity = max(1, block_total // dp_count)
    row_share = model_width // dp_count
    samples_all = S_DEV * dp_count
    grad_rows = lax.psum_scatter(
        lax.dot_general(
            activations, cotangent, (((0,), (0,)), ((), ())), preferred_element_type=jnp.float32
        ),
        "dp",
        scatter_dimension=0,
        tiled=True,
    )
    picked_acts = jnp.take(activations, sampled_rows, axis=0)
    picked_grads = jnp.take(cotangent, sampled_rows, axis=0)
    g_partial = lax.dot_general(
        picked_grads, picked_grads, (((0,), (0,)), ((), ())), preferred_element_type=jnp.float32
    )
    g_total = lax.psum(g_partial, "dp")
    g_factor = g_total * (tok_local / S_DEV) + DAMPING * jnp.eye(group_w, dtype=jnp.float32)
    slot_of = block_owner * capacity + block_rank(block_owner)
    dest_ids = jnp.arange(dp_count * capacity, dtype=jnp.int32)
    chooser = (slot_of[None, :] == dest_ids[:, None]).astype(jnp.bfloat16)
    row_blocks = picked_acts.reshape(S_DEV, block_total, FACTOR_BLOCK)
    outgoing = lax.dot_general(
        chooser, row_blocks, (((1,), (1,)), ((), ())), preferred_element_type=jnp.float32
    )
    outgoing = outgoing.astype(jnp.bfloat16).reshape(dp_count, capacity, S_DEV, FACTOR_BLOCK)
    gram_slots = owner_grams(
        lax.all_to_all(outgoing, "dp", split_axis=0, concat_axis=0, tiled=True)
    )
    a_factor = (
        gram_slots / samples_all + DAMPING * jnp.eye(FACTOR_BLOCK, dtype=jnp.float32)[None, :, :]
    )
    input_factor_inverse = newton_inverse(a_factor)
    owned_count = jnp.sum((block_owner == my_dp).astype(jnp.int32))
    slot_used = jnp.arange(capacity, dtype=jnp.int32) < owned_count
    owned_out = jnp.where(slot_used[:, None, None], input_factor_inverse, 0.0)
    g_inverse = newton_inverse(g_factor[None, :, :])[0]
    per_dev = max(1, row_share // FACTOR_BLOCK)
    rows_each = min(row_share, FACTOR_BLOCK)
    first_block = my_dp * row_share // FACTOR_BLOCK
    need_ids = first_block + jnp.arange(per_dev, dtype=jnp.int32)
    need_slots = jnp.take(slot_of, need_ids)
    row_offset = my_dp * row_share % FACTOR_BLOCK
    shard_piece = lax.all_gather(owned_out, "dp", axis=0, tiled=True)
    rows_part = lax.dynamic_slice_in_dim(shard_piece, row_offset, rows_each, 1)
    slot_ids = jnp.arange(shard_piece.shape[0], dtype=jnp.int32)
    selector = (need_slots[:, None] == slot_ids[None, :]).astype(jnp.float32)
    inverse_rows = jnp.einsum("jm,mkl->jkl", selector, rows_part, precision=precise_mode)
    grad_right = jnp.dot(
        grad_rows, g_inverse, precision=precise_mode, preferred_element_type=jnp.float32
    )
    partner = from_partner(grad_right, "dp", 0)
    is_lower = my_dp % 2 == 0
    joined = jnp.where(
        is_lower,
        jnp.concatenate([grad_right, partner], 0),
        jnp.concatenate([partner, grad_right], 0),
    )
    complete_rows = joined[None, :, :]
    natural_step = jnp.einsum("jrk,jkl->jrl", inverse_rows, complete_rows, precision=precise_mode)
    return (natural_step.reshape(row_share, group_w), owned_out)


def solution(mesh):
    return jax.shard_map(
        per_device,
        mesh=mesh,
        in_specs=(P("dp", None), P("dp", "tensor"), P("dp"), P()),
        out_specs=(P("dp", "tensor"), P("dp", None, None)),
        check_vma=False,
    )
```

profile of v0, /device:TPU:1, one launch (start us, length us, event | category | flops | bytes accessed | tf_op | source)
XLA Modules:
  0.0 975.9 jit_solution(2358637673614517384)
XLA Ops:
  7.2 0.7 compare_select_fusion
  7.9 0.7 compare_and_fusion
  8.6 0.7 gather_fusion.1
  9.3 1.0 fusion.37
  10.4 11.3 %fusion.52 = f32[8192,256]{1,0:T(8,128)} fusion(bf16[768,8192]{1,0:T(8,128)(2,1)} %param.8, bf16[768,256]{1,0:T(8,128)(2,1)S(1)} %copy-done), kind=kOutput, calls=%fused_computation.68 | convolution fusion | flops 3221225472 | bytes 21364736 | tf_op jit(solution)/shard_map/dot_general | solution.py:63
  21.7 8.4 gather_fusion
  30.5 0.6 fusion.47
  31.4 0.8 convert_bitcast_fusion
  32.2 2.5 copy.21
  34.7 10.3 %all-to-all-start = ((bf16[64,1,64,256]{3,2,1,0:T(8,128)(2,1)}), bf16[64,1,64,256]{3,2,1,0:T(8,128)(2,1)S(1)}, u32[]{:S(2)}, u32[]{:S(2)}) async-start(bf16[64,1,64,256]{3,2,1,0:T(8,128)(2,1)} %copy.21), calls=%async_computation | async-start | bytes 4194304 | tf_op jit(solution)/shard_map/all_to_all | solution.py:86
  45.9 29.0 %all-to-all-done = bf16[64,1,64,256]{3,2,1,0:T(8,128)(2,1)S(1)} async-done(((bf16[64,1,64,256]{3,2,1,0:T(8,128)(2,1)}), bf16[64,1,64,256]{3,2,1,0:T(8,128)(2,1)S(1)}, u32[]{:S(2)}, u32[]{:S(2)}) %all-to-all-start) | async-done | bytes 2097184 | tf_op jit(solution)/shard_map/all_to_all | solution.py:86
  74.9 0.9 abs_reduce_fusion.1
  75.9 0.7 reduce_max.18
  77.6 10.7 %while.23 = (s32[]{:T(128)}, f32[1,256,256]{1,2,0:T(8,128)S(1)}, f32[1,256,256]{2,1,0:T(8,128)S(1)}, s32[]{:T(128)}) while((s32[]{:T(128)}, f32[1,256,256]{1,2,0:T(8,128)S(1)}, f32[1,256,256]{2,1,0:T(8,128)S(1)}, s32[]{:T(128)}) %tuple.58), condition=%wide.region_5.6_spmd.clone, body=%wide.region_4.5_spmd.clone.sunk | while | flops 402849792 | bytes 2097205 | solution.py:37
  78.0 0.6 convolution_bitcast_fusion.4
  79.1 0.6 convolution_bitcast_fusion.4
  79.8 0.4 convolution_subtract_fusion.4
  80.2 0.6 convolution_bitcast_fusion.4
  81.2 0.6 convolution_bitcast_fusion.4
  82.3 0.6 convolution_bitcast_fusion.4
  83.4 0.6 convolution_bitcast_fusion.4
  84.5 0.6 convolution_bitcast_fusion.4
  85.5 0.6 convolution_bitcast_fusion.4
  86.6 0.6 convolution_bitcast_fusion.4
  87.7 0.6 convolution_bitcast_fusion.4
  88.4 0.7 broadcast_select_fusion
  89.2 0.7 dynamic-slice.2
  90.5 438.1 %all-reduce.2.cloned.1.call-done = f32[256,256]{0,1:T(8,128)} async-done(((f32[256,256]{0,1:T(8,128)}), f32[256,256]{0,1:T(8,128)}) %all-reduce.2.cloned.1.call-update) | async-done | bytes 262160 | tf_op jit(solution)/shard_map/psum | solution.py:75
  528.6 1.0 fusion.33
  529.6 0.6 reduce_max.19
  531.1 10.7 %while.24 = (s32[]{:T(128)}, f32[1,256,256]{1,2,0:T(8,128)S(1)}, f32[1,256,256]{2,1,0:T(8,128)S(1)}, s32[]{:T(128)}) while((s32[]{:T(128)}, f32[1,256,256]{1,2,0:T(8,128)S(1)}, f32[1,256,256]{2,1,0:T(8,128)S(1)}, s32[]{:T(128)}) %tuple.55), condition=%wide.region_11.12_spmd.clone, body=%wide.region_10.11_spmd.clone.sunk | while | flops 402849792 | bytes 2097205 | solution.py:37
  531.6 0.6 convolution_bitcast_fusion.5
  532.6 0.6 convolution_bitcast_fusion.5
  533.7 0.6 convolution_bitcast_fusion.5
  534.8 0.6 convolution_bitcast_fusion.5
  535.8 0.6 convolution_bitcast_fusion.5
  536.9 0.6 convolution_bitcast_fusion.5
  538.0 0.6 convolution_bitcast_fusion.5
  539.1 0.6 convolution_bitcast_fusion.5
  540.1 0.6 convolution_bitcast_fusion.5
  541.2 0.6 convolution_bitcast_fusion.5
  541.8 286.0 %reduce-scatter.2.cloned.1.call-done = f32[128,256]{1,0:T(8,128)} async-done(((f32[8192,256]{1,0:T(8,128)}), f32[128,256]{1,0:T(8,128)}) %reduce-scatter.2.cloned.1.call-update) | async-done | bytes 131088 | tf_op jit(solution)/shard_map/reduce_scatter | solution.py:62
  827.8 1.3 fusion.29
  829.1 6.3 collective-permute-start
  835.4 121.7 %all-gather.2.cloned.1.call-done = f32[64,256,256]{2,1,0:T(8,128)} async-done(((f32[1,256,256]{2,1,0:T(8,128)}), f32[64,256,256]{2,1,0:T(8,128)}) %all-gather.2.cloned.1.call-update) | async-done | bytes 16777232 | tf_op jit(solution)/shard_map/all_gather | solution.py:102
  957.0 3.9 constant_dynamic-slice_fusion
  961.0 7.5 fusion.10
  968.5 0.9 fusion.23
  (61 shorter events, 10.0 us)
Async XLA Ops:
  7.2 1.4 copy-start
  7.2 521.4 %all-reduce.2.cloned.1.call-start = ((), (), s32[]{:S(2)}) async-start(), calls=%async_computation.4 | async-start | bytes 524288 | tf_op jit(solution)/shard_map/psum | solution.py:75
  10.3 817.5 %reduce-scatter.2.cloned.1.call-start = ((), (), s32[]{:S(2)}) async-start(), calls=%async_computation.3 | async-start | bytes 8519680 | tf_op jit(solution)/shard_map/reduce_scatter | solution.py:62
  21.7 8.7 copy-start.1
  34.7 40.2 %all-to-all-start = ((bf16[64,1,64,256]{3,2,1,0:T(8,128)(2,1)}), bf16[64,1,64,256]{3,2,1,0:T(8,128)(2,1)S(1)}, u32[]{:S(2)}, u32[]{:S(2)}) async-start(bf16[64,1,64,256]{3,2,1,0:T(8,128)(2,1)} %copy.21), calls=%async_computation | async-start | bytes 4194304 | tf_op jit(solution)/shard_map/all_to_all | solution.py:86
  45.1 912.0 %all-gather.2.cloned.1.call-start = ((), (), s32[]{:S(2)}) async-start(), calls=%async_computation.2 | async-start | bytes 17039360 | tf_op jit(solution)/shard_map/all_gather | solution.py:102
  829.1 139.4 %collective-permute-start = (f32[128,256]{1,0:T(8,128)S(1)}, f32[128,256]{1,0:T(8,128)S(1)}, u32[]{:S(2)}, u32[]{:S(2)}) collective-permute-start(f32[128,256]{1,0:T(8,128)S(1)} %fusion.29), channel_id=1, source_target_pairs={{0,4},{4,0},{8,12},{12,8},{16,20},{20,16},{24,28},{28,24},{32,36},... | collective-permute-start | bytes 393224 | tf_op jit(solution)/shard_map/ppermute | solution.py:22
Sparse Core Ops, SparseCore 0:
  10.6 517.9 all-reduce.1
  531.1 296.6 reduce-scatter.1
  830.2 126.7 all-gather.1
where the time goes:
time: 976 us
  waiting for transfers between devices  875 us (90%)
  matrix products  44 us (5%)
  local copies, waits for them, and re-layouts  17.5 us (2%)
  starting transfers between devices  16.9 us (2%)
  between operations  16.6 us (2%)
    psum x1, waiting for transfers between devices, per_device(): g_total = lax.psum(g_partial, 'dp')  438 us
    reduce_scatter x1, waiting for transfers between devices, per_device(): lax.psum_scatter(lax.dot_general(activations, cotangent, (((0,), (0,)), (...  286 us
    all_gather x1, waiting for transfers between devices, per_device(): shard_piece = lax.all_gather(owned_out, 'dp', axis=0, tiled=True)  122 us
    all_to_all x1, waiting for transfers between devices, per_device(): lax.all_to_all(outgoing, 'dp', split_axis=0, concat_axis=0, tiled=True)  29 us
  transfers between devices with their start and end apart: 5, of which 4 were waited for; matrix products, arithmetic and copies ran while one was open for 6% of the time, Pallas kernels for 0%

commit v1 on v0

v1 whole, which is shorter than its diff:
```python
import jax
import jax.numpy as jnp
from jax import lax
from jax.experimental import pallas as pl
from jax.experimental.pallas import tpu as pltpu
from jax.sharding import PartitionSpec as P

S_DEV = 64
BLK = 256
HALF = 128
ITERS = 10
DAMPING = 0.05
MESH = pl.DeviceIdType.MESH
HI = lax.Precision.HIGHEST
F32 = jnp.float32
BF16 = jnp.bfloat16


class Sems:
    def __init__(self, send, recv):
        self.send, self.recv, self.used = send, recv, 0

    def take(self, count):
        base = self.used
        self.used += count
        return base


SEM_TOTAL = 128


def dot_hi(a, b, dims=(((1,), (0,)), ((), ()))):
    return lax.dot_general(a, b, dims, precision=HI, preferred_element_type=F32)


def gram(rows):
    return lax.dot_general(rows, rows, (((0,), (0,)), ((), ())), preferred_element_type=F32)


def eye(n):
    r = lax.broadcasted_iota(jnp.int32, (n, n), 0)
    c = lax.broadcasted_iota(jnp.int32, (n, n), 1)
    return jnp.where(r == c, 1.0, 0.0).astype(F32)


def newton_inverse(m_ref, x_ref, e_ref):
    ident = eye(BLK)
    m = m_ref[...]
    bound = jnp.max(jnp.sum(jnp.abs(m), axis=1, keepdims=True), axis=0, keepdims=True)
    inv = 1.0 / bound
    e_ref[...] = ident - m * inv
    x_ref[...] = (ident + e_ref[...]) * inv
    e = e_ref[...]
    e_ref[...] = dot_hi(e, e)

    def step(k, _):
        e = e_ref[...]
        x = x_ref[...]
        both = dot_hi(jnp.concatenate([x, e], axis=0), e)
        x_ref[...] = x + both[:BLK]
        e_ref[...] = both[BLK:]
        return 0

    lax.fori_loop(0, 4, step, 0)
    e_ref[...] = ident - dot_hi(m, x_ref[...])
    lax.fori_loop(0, 4, step, 0)
    x_ref[...] += dot_hi(x_ref[...], e_ref[...])


def kernel(
    act_hbm, cot_ref, rows_ref, owned_ref,
    step_out, slot_out,
    act, lhs, buf, pairs, rs1, acc1, rs2, acc2, rs3, fin,
    picks, pg, r1, r2, g1, g2,
    gr, gx, gh, gz, need, m_ref, x_ref, e_ref, inv,
    s1, s2, dd, t1, t2, outh,
    act_sem, send_sem, recv_sem,
):
    dp = lax.axis_index("dp")
    c = lax.rem(dp, 2)
    z = lax.rem(lax.div(dp, 2), 2)
    y = lax.rem(lax.div(dp, 4), 4)
    x = lax.div(dp, 16)
    u = (1 - c) * x + c * y
    v = (1 - c) * y + c * x
    oc = 1 - c
    oz = 1 - z

    def dev(xx, yy, zz, cc):
        return ((xx * 4 + yy) * 2 + zz) * 2 + cc

    def dev_uv(uu, vv, cc):
        return dev((1 - c) * uu + c * vv, (1 - c) * vv + c * uu, z, cc)

    def wrap(a):
        return lax.rem(a, 4)

    def peer_u(k):
        return dev_uv(wrap(u + k), v, c)

    def peer_v(k):
        return dev_uv(u, wrap(v + k), c)

    peer_z = dev(x, y, oz, c)
    peer_c = dev(x, y, z, oc)

    def pair_of(uu, vv):
        return (1 - c) * (uu * 4 + vv) + c * (vv * 4 + uu)

    sems = Sems(send_sem, recv_sem)

    def rcopy(src, dst, send_i, recv_i, to):
        return pltpu.make_async_remote_copy(
            src_ref=src, dst_ref=dst, send_sem=send_sem.at[send_i], recv_sem=recv_sem.at[recv_i],
            device_id={"dp": to}, device_id_type=MESH,
        )

    def act_copy(i, p):
        cols = pl.ds(pl.multiple_of(p * 2 * BLK, 2 * BLK), 2 * BLK)
        return pltpu.make_async_copy(act_hbm.at[:, cols], act.at[:, cols], act_sem.at[i])

    def visit(i):
        a, b = lax.div(i, 4), lax.rem(i, 4)
        g = wrap(x + wrap(a + 1))
        j = wrap(y + wrap(b + 1))
        uu = (1 - c) * g + c * j
        vv = (1 - c) * j + c * g
        return g * 4 + j, uu, vv, wrap(uu - u + 4)

    def start_load(i, _):
        act_copy(i, visit(i)[0]).start()
        return 0

    lax.fori_loop(0, 16, start_load, 0)

    barrier = pltpu.get_barrier_semaphore()
    for to in [peer_u(1), peer_u(2), peer_u(3), peer_v(1), peer_v(2), peer_v(3), peer_z, peer_c]:
        pl.semaphore_signal(barrier, inc=1, device_id={"dp": to}, device_id_type=MESH)

    lhs[0:BLK, :] = cot_ref[...].T
    tok = lax.broadcasted_iota(jnp.int32, (S_DEV, lhs.shape[1]), 1)
    onehot = (tok == rows_ref[...]).astype(F32).astype(BF16)
    lhs[BLK:, :] = onehot
    pg[...] = jnp.dot(onehot, cot_ref[...], preferred_element_type=F32).astype(BF16)
    s2[2, 0, 0, :, :] = jnp.zeros((8, BLK), F32)

    pl.semaphore_wait(barrier, 8)

    pick_b = sems.take(16)
    pair_b = sems.take(16)
    rs1_b = sems.take(16)
    rows2_b = sems.take(4)
    g1_b = sems.take(4)
    g2_b = sems.take(4)
    rs2_b = sems.take(4)
    rs3_b = sems.take(1)
    rs4_b = sems.take(1)
    gx_b = sems.take(1)
    gz_b = sems.take(2)
    need_b = sems.take(1)
    inv_b = sems.take(1)
    s1_b = sems.take(4)
    s2_b = sems.take(4)
    s3_b = sems.take(1)
    t1_b = sems.take(4)
    t2_b = sems.take(4)
    out_b = sems.take(1)

    def g1_copy(k):
        return rcopy(pg, g1.at[k], g1_b + k, g1_b + k, peer_u(k))

    for k in (2, 1, 3):
        g1_copy(k).start()

    def pick_copy(i, p, uu, vv, k):
        return rcopy(
            picks.at[:, p], r1.at[:, vv, k], pick_b + i, pick_b + vv * 4 + k, dev_uv(uu, v, c)
        )

    def pair_copy(i, p):
        return rcopy(buf.at[oc, p], pairs.at[p], pair_b + i, pair_b + p, peer_c)

    def rs1_copy(i, p, uu, vv, k):
        return rcopy(
            buf.at[c, p], rs1.at[k - 1, vv], rs1_b + i, rs1_b + vv * 4 + k, dev_uv(uu, v, c)
        )

    def body(i, _):
        @pl.when(i < 16)
        def _():
            p, uu, vv, k = visit(i)
            act_copy(i, p).wait()
            cols = pl.ds(pl.multiple_of(p * 2 * BLK, 2 * BLK), 2 * BLK)
            res = jnp.dot(lhs[...], act[:, cols], preferred_element_type=F32)
            for h in range(2):
                for zz in range(2):
                    buf[h, p, zz, :, :] = res[h * HALF:(h + 1) * HALF, zz * BLK:(zz + 1) * BLK]
            for zz in range(2):
                picks[zz, p, :, :] = res[BLK:, zz * BLK:(zz + 1) * BLK].astype(BF16)
            pair_copy(i, p).start()

            @pl.when(k != 0)
            def _():
                pick_copy(i, p, uu, vv, k).start()

            @pl.when(k == 0)
            def _():
                r1[:, vv, 0, :, :] = picks[:, p, :, :]

        @pl.when(i >= 3)
        def _():
            p, uu, vv, k = visit(i - 3)
            pair_copy(i - 3, p).wait_recv()
            buf[c, p, :, :, :] = buf[c, p, :, :, :] + pairs[p, :, :, :]

            @pl.when(k != 0)
            def _():
                rs1_copy(i - 3, p, uu, vv, k).start()

        return 0

    lax.fori_loop(0, 19, body, 0)

    for k in (2, 1, 3):
        g1_copy(k).wait_recv()
    g1[0, :, :] = pg[...]

    def g2_copy(k):
        return rcopy(g1, g2.at[k], g2_b + k, g2_b + k, peer_v(k))

    def rows2_copy(k):
        return rcopy(r1.at[:, wrap(v + k)], r2.at[:, k], rows2_b + k, rows2_b + k, peer_v(k))

    def pick_wait(vv, k):
        rcopy(picks.at[:, 0], r1.at[:, vv, k], pick_b, pick_b + vv * 4 + k, peer_u(k)).wait_recv()

    for k in (2, 1, 3):
        for kk in (1, 2, 3):
            pick_wait(wrap(v + k), kk)
        rows2_copy(k).start()
        g2_copy(k).start()
    for kk in (1, 2, 3):
        pick_wait(v, kk)

    for zz in range(2):
        got = gram(r1[zz, v, :, :, :].reshape(4 * S_DEV, BLK))
        gr[zz, 0, :, :] = got[:HALF]
        gr[zz, 1, :, :] = got[HALF:]
    got = gram(g1[...].reshape(4 * S_DEV, BLK))
    gr[2, 0, :, :] = got[:HALF]
    gr[2, 1, :, :] = got[HALF:]
    for k in (1, 3, 2):
        rows2_copy(k).wait_recv()
        g2_copy(k).wait_recv()
        for zz in range(3):
            if zz < 2:
                got = gram(r2[zz, k, :, :, :].reshape(4 * S_DEV, BLK))
            else:
                got = gram(g2[k, :, :, :].reshape(4 * S_DEV, BLK))
            gr[zz, 0, :, :] += got[:HALF]
            gr[zz, 1, :, :] += got[HALF:]
    gx_copy = rcopy(gr.at[:, oc], gx, gx_b, gx_b, peer_c)
    gx_copy.start()
    gx_copy.wait_recv()
    gh[...] = gr[:, c, :, :] + gx[...]
    gz_copies = [
        rcopy(gh.at[oz], gz.at[0], gz_b, gz_b, peer_z),
        rcopy(gh.at[2], gz.at[1], gz_b + 1, gz_b + 1, peer_z),
    ]
    for copy in gz_copies:
        copy.start()
    for copy in gz_copies:
        copy.wait_recv()
    need[0, c, :, :] = gh[z, :, :] + gz[0, :, :]
    need[1, c, :, :] = gh[2, :, :] + gz[1, :, :]
    need_copy = rcopy(need.at[oc, c], need.at[oc, c], need_b, need_b, peer_c)
    need_copy.start()
    need_copy.wait_recv()
    cf = c.astype(F32)
    scale = (1.0 - cf) / 4096.0 + cf * 12.0
    m_ref[...] = need[c, :, :, :].reshape(BLK, BLK) * scale + DAMPING * eye(BLK)
    newton_inverse(m_ref, x_ref, e_ref)
    inv[c, :, :, :, :, :] = x_ref[...].reshape(2, 4, 4, 8, BLK)
    inv_copy = rcopy(inv.at[c], inv.at[c], inv_b, inv_b, peer_c)
    inv_copy.start()

    def rs1_wait(vv, k):
        rcopy(
            buf.at[c, 0], rs1.at[k - 1, vv], rs1_b, rs1_b + vv * 4 + k, peer_u(k)
        ).wait_recv()

    def rs2_copy(k):
        return rcopy(
            acc1.at[wrap(v + k)], rs2.at[k], rs2_b + k, rs2_b + k, peer_v(k)
        )

    for k in (2, 1, 3, 0):
        vv = wrap(v + k)
        for kk in (1, 2, 3):
            rs1_wait(vv, kk)
        acc1[vv, :, :, :] = (
            buf[c, pair_of(u, vv), :, :, :] + rs1[0, vv, :, :, :]
            + rs1[1, vv, :, :, :] + rs1[2, vv, :, :, :]
        )
        if k:
            rs2_copy(k).start()

    inv_copy.wait_recv()

    def s1_copy(k):
        return rcopy(inv.at[0, c, wrap(u + k)], s1.at[k], s1_b + k, s1_b + k, peer_u(k))

    for k in (2, 1, 3):
        s1_copy(k).start()
    s1[0, :, :, :] = inv[0, c, u, :, :, :]
    for k in (1, 3, 2):
        s1_copy(k).wait_recv()

    def s2_copy(k):
        return rcopy(
            s1.at[:, wrap(v + k)], s2.at[0, k], s2_b + k, s2_b + k, peer_v(k)
        )

    for k in (2, 1, 3):
        s2_copy(k).start()
    s2[0, 0, :, :, :] = s1[:, v, :, :]
    for k in (1, 3, 2):
        s2_copy(k).wait_recv()
    s3_copy = rcopy(s2.at[0], s2.at[1], s3_b, s3_b, peer_z)
    s3_copy.start()

    for k in (1, 3, 2):
        rs2_copy(k).wait_recv()
    acc2[...] = acc1[v, :, :, :] + rs2[1, :, :, :] + rs2[2, :, :, :] + rs2[3, :, :, :]
    rs3_copy = rcopy(acc2.at[oz], rs3, rs3_b, rs3_b, peer_z)
    rs3_copy.start()

    s3_copy.wait_recv()
    for kv in range(4):
        for ku in range(4):
            for cc in range(2):
                b = owned_ref[dev_uv(wrap(u + ku), wrap(v + kv), cc)]
                bb = jnp.maximum(b, 0)
                bz = lax.rem(bb, 2)
                by = lax.rem(lax.div(bb, 2), 4)
                bx = lax.div(bb, 8)
                bu = (1 - c) * bx + c * by
                bv = (1 - c) * by + c * bx
                hop = wrap(bz - z + 4)
                zi = lax.rem(hop, 2)
                none = b < 0
                i0 = jnp.where(none, 2, zi)
                i1 = jnp.where(none, 0, wrap(v - bv + 4))
                i2 = jnp.where(none, 0, wrap(u - bu + 4))
                dd[kv, ku, cc, :, :] = s2[i0, i1, i2, :, :]

    def t1_copy(k):
        return rcopy(dd.at[k], t1.at[k], t1_b + k, t1_b + k, peer_v(k))

    for k in (2, 1, 3):
        t1_copy(k).start()
    t1[0, :, :, :, :] = dd[0, :, :, :, :]

    rs3_copy.wait_recv()
    fin[c, :, :] = acc2[z, :, :] + rs3[...]
    rs4_copy = rcopy(fin.at[c], fin.at[c], rs4_b, rs4_b, peer_c)
    rs4_copy.start()

    for k in (1, 3, 2):
        t1_copy(k).wait_recv()

    def t2_copy(k):
        return rcopy(t1.at[:, k], t2.at[k], t2_b + k, t2_b + k, peer_u(k))

    for k in (2, 1, 3):
        t2_copy(k).start()
    t2[0, :, :, :, :] = t1[:, 0, :, :, :]

    rs4_copy.wait_recv()
    left = dot_hi(
        inv[0, c, :, :, :, :].reshape(HALF, BLK), fin[...].reshape(BLK, BLK), (((1,), (1,)), ((), ()))
    )
    step_out[...] = dot_hi(left, inv[1, :, :, :, :, :].reshape(BLK, BLK))

    for k in (1, 3, 2):
        t2_copy(k).wait_recv()
    for ku in range(4):
        for kv in range(4):
            row = wrap(u - ku + 4) * 4 + wrap(v - kv + 4)
            for cc in range(2):
                outh[cc, 0, row, :, :] = t2[ku, kv, cc, :, :]
    out_copy = rcopy(outh.at[oc, 0], outh.at[oc, 1], out_b, out_b, peer_c)
    out_copy.start()
    out_copy.wait_recv()
    slot_out[0, pl.ds(pl.multiple_of(c * HALF, HALF), HALF), :] = outh[c, 0, :, :, :].reshape(HALF, BLK)
    slot_out[0, pl.ds(pl.multiple_of(oc * HALF, HALF), HALF), :] = outh[c, 1, :, :, :].reshape(HALF, BLK)

    def drain(i, _):
        p, uu, vv, k = visit(i)
        pair_copy(i, p).wait_send()

        @pl.when(k != 0)
        def _():
            pick_copy(i, p, uu, vv, k).wait_send()
            rs1_copy(i, p, uu, vv, k).wait_send()

        return 0

    lax.fori_loop(0, 16, drain, 0)
    for k in (1, 2, 3):
        for make in (g1_copy, g2_copy, rows2_copy, rs2_copy, s1_copy, s2_copy, t1_copy, t2_copy):
            make(k).wait_send()
    for copy in [gx_copy, *gz_copies, need_copy, inv_copy, s3_copy, rs3_copy, rs4_copy, out_copy]:
        copy.wait_send()


def per_device(activations, cotangent, sampled_rows, block_owner):
    tokens, width = activations.shape
    ids = jnp.arange(64, dtype=jnp.int32)
    blocks = jnp.arange(block_owner.shape[0], dtype=jnp.int32)
    owned = jnp.max(
        jnp.where(block_owner[None, :] == ids[:, None], blocks[None, :], -1), axis=1
    )
    vmem = pltpu.VMEM
    return pl.pallas_call(
        kernel,
        out_shape=(
            jax.ShapeDtypeStruct((HALF, BLK), F32),
            jax.ShapeDtypeStruct((1, BLK, BLK), F32),
        ),
        in_specs=[
            pl.BlockSpec(memory_space=pl.ANY),
            pl.BlockSpec(memory_space=pltpu.VMEM),
            pl.BlockSpec(memory_space=pltpu.VMEM),
            pl.BlockSpec(memory_space=pltpu.SMEM),
        ],
        out_specs=(
            pl.BlockSpec(memory_space=pltpu.VMEM),
            pl.BlockSpec(memory_space=pltpu.VMEM),
        ),
        scratch_shapes=[
            vmem((tokens, width), BF16),
            vmem((BLK + S_DEV, tokens), BF16),
            vmem((2, 16, 2, HALF, BLK), F32),
            vmem((16, 2, HALF, BLK), F32),
            vmem((3, 4, 2, HALF, BLK), F32),
            vmem((4, 2, HALF, BLK), F32),
            vmem((4, 2, HALF, BLK), F32),
            vmem((2, HALF, BLK), F32),
            vmem((HALF, BLK), F32),
            vmem((2, HALF, BLK), F32),
            vmem((2, 16, S_DEV, BLK), BF16),
            vmem((S_DEV, BLK), BF16),
            vmem((2, 4, 4, S_DEV, BLK), BF16),
            vmem((2, 4, 4, S_DEV, BLK), BF16),
            vmem((4, S_DEV, BLK), BF16),
            vmem((4, 4, S_DEV, BLK), BF16),
            vmem((3, 2, HALF, BLK), F32),
            vmem((3, HALF, BLK), F32),
            vmem((3, HALF, BLK), F32),
            vmem((2, HALF, BLK), F32),
            vmem((2, 2, HALF, BLK), F32),
            vmem((BLK, BLK), F32),
            vmem((BLK, BLK), F32),
            vmem((BLK, BLK), F32),
            vmem((2, 2, 4, 4, 8, BLK), F32),
            vmem((4, 4, 8, BLK), F32),
            vmem((3, 4, 4, 8, BLK), F32),
            vmem((4, 4, 2, 8, BLK), F32),
            vmem((4, 4, 2, 8, BLK), F32),
            vmem((4, 4, 2, 8, BLK), F32),
            vmem((2, 2, 16, 8, BLK), F32),
            pltpu.SemaphoreType.DMA((16,)),
            pltpu.SemaphoreType.DMA((SEM_TOTAL,)),
            pltpu.SemaphoreType.DMA((SEM_TOTAL,)),
        ],
        compiler_params=pltpu.CompilerParams(
            collective_id=0, has_side_effects=True, vmem_limit_bytes=60 * 1024 * 1024
        ),
    )(activations, cotangent, sampled_rows.reshape(S_DEV, 1), owned)


def solution(mesh):
    return jax.shard_map(
        per_device,
        mesh=mesh,
        in_specs=(P("dp", None), P("dp", "tensor"), P("dp"), P()),
        out_specs=(P("dp", "tensor"), P("dp", None, None)),
        check_vma=False,
    )
```

time: 976 us -> 98 us (0.10)
  waiting for transfers between devices: 875 us -> 0 us
  Pallas kernels: 0 us -> 91.3 us
  matrix products: 44 us -> 0 us
  starting transfers between devices: 16.9 us -> 0 us
  between operations: 16.6 us -> 0.64 us
  local copies, waits for them, and re-layouts: 17.5 us -> 4.59 us
    psum x1 -> x0, waiting for transfers between devices: 438 us -> none  [per_device(): g_total = lax.psum(g_partial, 'dp')]
    reduce_scatter x1 -> x0, waiting for transfers between devices: 286 us -> none  [per_device(): lax.psum_scatter(lax.dot_general(activations, cotangent, (((0,), (0,)), (...]
    all_gather x1 -> x0, waiting for transfers between devices: 122 us -> none  [per_device(): shard_piece = lax.all_gather(owned_out, 'dp', axis=0, tiled=True)]
    pallas_call x0 -> x1, Pallas kernels: none -> 91.3 us  [per_device(): pl.pallas_call(kernel, out_shape=(jax.ShapeDtypeStruct((HALF, BLK), F32),...]
    dot_general x47 -> x0, matrix products: 44 us -> none  [the longest x20 11.9 us: advance(): jnp.einsum('nij,njk->nik', current, 2.0 * identity[None, :, :] - product,...]
    all_to_all x1 -> x0, waiting for transfers between devices: 29 us -> none  [per_device(): lax.all_to_all(outgoing, 'dp', split_axis=0, concat_axis=0, tiled=True)]
    all_to_all x1 -> x0, starting transfers between devices: 10.3 us -> none  [per_device(): lax.all_to_all(outgoing, 'dp', split_axis=0, concat_axis=0, tiled=True)]
  transfers between devices with their start and end apart: 5 -> 0, of which waited for: 4 -> 0; matrix products, arithmetic and copies ran while one was open for 6% -> 0% of each run, Pallas kernels for 0% -> 0%
where the time goes in v1:
time: 98 us; the launch traced here: 97.8 us
  Pallas kernels  91.3 us (93%)
  local copies, waits for them, and re-layouts  4.59 us (5%)
  other arithmetic  1.25 us (1%)
    pallas_call x1, Pallas kernels, per_device(): pl.pallas_call(kernel, out_shape=(jax.ShapeDtypeStruct((HALF, BLK), F32),...  91.3 us
    unnamed x2, local copies, waits for them, and re-layouts  3.24 us

profile of v1, /device:TPU:1, one launch (start us, length us, event | category | flops | bytes accessed | tf_op | source)
XLA Modules:
  0.0 97.8 jit_solution(17900684502075477832)
XLA Ops:
  0.6 1.3 %select_reduce_fusion.owned_ref = s32[64]{0:T(128)} fusion(s32[32]{0:T(128)} %param.7), kind=kLoop, calls=%fused_computation | loop fusion | flops 6080 | bytes 384 | tf_op jit(solution)/shard_map/reduce_max | solution.py:421
  1.9 1.4 %copy.7.rows_ref = s32[64,1]{1,0:T(8,128)} copy(s32[64,1]{0,1:T(1,128)} %bitcast.1) | data formatting | bytes 512 | tf_op jit(solution)/shard_map/reshape | solution.py:480
  3.2 91.3 %shard_map.59 = (f32[128,256]{1,0:T(8,128)}, f32[1,256,256]{2,1,0:T(8,128)}) custom-call(bf16[768,8192]{1,0:T(8,128)(2,1)} %act_hbm.1, bf16[768,256]{1,0:T(8,128)(2,1)} %cot_ref.1, s32[64,1]{1,0:T(8,128)} %copy.7.rows_ref, s32[64]{0:T(128)} %select_reduce_fusion.owned_ref), custom_call_target="tpu_custom_call" | custom-call | tf_op jit(solution)/shard_map/pallas_call | solution.py:425
  94.5 1.6 %copy.10 = f32[128,256]{1,0:T(8,128)} copy(f32[128,256]{1,0:T(8,128)} %get-tuple-element.4) | data formatting | bytes 262144
  96.1 1.7 %copy.11 = f32[1,256,256]{2,1,0:T(8,128)} copy(f32[1,256,256]{2,1,0:T(8,128)} %get-tuple-element.5) | data formatting | bytes 524288

commit v2 on v0

v2 whole, which is shorter than its diff:
```python
import jax
import jax.numpy as jnp
from jax import lax
from jax.experimental import pallas as pl
from jax.experimental.pallas import tpu as pltpu
from jax.sharding import PartitionSpec as P

S_DEV = 64
BLK = 256
HALF = 128
ITERS = 10
DAMPING = 0.05
MESH = pl.DeviceIdType.MESH
HI = lax.Precision.HIGHEST
F32 = jnp.float32
BF16 = jnp.bfloat16


class Sems:
    def __init__(self):
        self.used = 0

    def take(self, count):
        base = self.used
        self.used += count
        return base


SEM_TOTAL = 144
LAG = 3
REL_EARLY = 2
GRAD_ORDER = (
    (2, 2), (2, 1), (1, 2), (2, 3), (3, 2), (2, 0), (0, 2),
    (1, 1), (1, 3), (3, 1), (3, 3), (1, 0), (0, 1), (3, 0), (0, 3), (0, 0),
)


def dot_hi(a, b, dims=(((1,), (0,)), ((), ()))):
    return lax.dot_general(a, b, dims, precision=HI, preferred_element_type=F32)


def gram(rows):
    return lax.dot_general(rows, rows, (((0,), (0,)), ((), ())), preferred_element_type=F32)


def eye(n):
    r = lax.broadcasted_iota(jnp.int32, (n, n), 0)
    c = lax.broadcasted_iota(jnp.int32, (n, n), 1)
    return jnp.where(r == c, 1.0, 0.0).astype(F32)


def newton_step(x_ref, e_ref):
    def step(k, _):
        e = e_ref[...]
        x = x_ref[...]
        both = dot_hi(jnp.concatenate([x, e], axis=0), e)
        x_ref[...] = x + both[:BLK]
        e_ref[...] = both[BLK:]
        return 0

    return step


def newton_begin(m_ref, x_ref, e_ref):
    ident = eye(BLK)
    m = m_ref[...]
    bound = jnp.max(jnp.sum(jnp.abs(m), axis=1, keepdims=True), axis=0, keepdims=True)
    inv = 1.0 / bound
    e = ident - m * inv
    x_ref[...] = (ident + e) * inv
    e_ref[...] = dot_hi(e, e)
    lax.fori_loop(0, 4, newton_step(x_ref, e_ref), 0)
    e_ref[...] = ident - dot_hi(m, x_ref[...])


def newton_end(x_ref, e_ref):
    lax.fori_loop(0, 4, newton_step(x_ref, e_ref), 0)
    x_ref[...] += dot_hi(x_ref[...], e_ref[...])


def kernel(
    act_hbm, cot_hbm, rows_ref, owner_ref,
    step_hbm, slot_hbm,
    act, cot_ref, cott, onehot, buf, pairs, rel, rs1, acc1, rs2, acc2, rs3, fin,
    picks, pg, r1, r2, g1, g2,
    gr, gx, gh, gz, m_ref, x_ref, e_ref, isl, isx, ginv,
    ss, dd, tt, outh, slot_v, step_v, table,
    act_sem, out_sem, send_sem, recv_sem,
):
    dp = lax.axis_index("dp")
    ten = lax.axis_index("tensor")
    c = lax.rem(dp, 2)
    z = lax.rem(lax.div(dp, 2), 2)
    y = lax.rem(lax.div(dp, 4), 4)
    x = lax.div(dp, 16)
    u = (1 - c) * x + c * y
    v = (1 - c) * y + c * x
    oc = 1 - c
    oz = 1 - z

    def wrap(a):
        return lax.rem(a, 4)

    def dev(xx, yy, zz, cc):
        return ((xx * 4 + yy) * 2 + zz) * 2 + cc

    def dev_uv(uu, vv, cc):
        return dev((1 - c) * uu + c * vv, (1 - c) * vv + c * uu, z, cc)

    def at(d):
        return {"dp": d, "tensor": ten}

    def peer_u(k):
        return at(dev_uv(wrap(u + k), v, c))

    def peer_v(k):
        return at(dev_uv(u, wrap(v + k), c))

    peer_z = at(dev(x, y, oz, c))
    peer_w = {"dp": dev(x, y, oz, c), "tensor": wrap(ten + 3 + 2 * z)}
    peer_c = at(dev(x, y, z, oc))

    def pair_of(uu, vv):
        return (1 - c) * (uu * 4 + vv) + c * (vv * 4 + uu)

    sems = Sems()

    def rcopy(src, dst, send_i, recv_i, to):
        return pltpu.make_async_remote_copy(
            src_ref=src, dst_ref=dst, send_sem=send_sem.at[send_i], recv_sem=recv_sem.at[recv_i],
            device_id=to, device_id_type=MESH,
        )

    def columns(p):
        return pl.ds(pl.multiple_of(p * 2 * BLK, 2 * BLK), 2 * BLK)

    def act_copy(i, p):
        return pltpu.make_async_copy(act_hbm.at[:, columns(p)], act.at[:, columns(p)], act_sem.at[i])

    def visit(i):
        g = wrap(x + wrap(lax.div(i, 4) + 1))
        j = wrap(y + wrap(lax.rem(i, 4) + 1))
        uu = (1 - c) * g + c * j
        vv = (1 - c) * j + c * g
        return g * 4 + j, uu, vv, wrap(uu - u + 4)

    def start_load(i, _):
        act_copy(i, visit(i)[0]).start()
        return 0

    lax.fori_loop(0, 16, start_load, 0)
    cot_copy = pltpu.make_async_copy(cot_hbm, cot_ref, act_sem.at[16])
    cot_copy.start()

    barrier = pltpu.get_barrier_semaphore()

    def chip(n):
        dz, dx, dy = lax.div(n, 16), lax.rem(lax.div(n, 4), 4), lax.rem(n, 4)
        xx, yy, zz = wrap(x + dx), wrap(y + dy), lax.rem(z + dz, 2)
        return xx, yy, zz, dz, dx, dy

    def chip_dev(n):
        xx, yy, zz, dz, dx, dy = chip(n)
        other = dz * lax.rem(dx + dy, 2)
        return {"dp": dev(xx, yy, zz, c), "tensor": wrap(ten + other * (3 + 2 * z))}

    def greet(n, _):
        pl.semaphore_signal(barrier, inc=1, device_id=chip_dev(n), device_id_type=MESH)
        return 0

    lax.fori_loop(1, 32, greet, 0)
    for to in [peer_w, peer_c]:
        pl.semaphore_signal(barrier, inc=1, device_id=to, device_id_type=MESH)

    r_i = lax.broadcasted_iota(jnp.int32, (S_DEV, S_DEV), 0)
    c_i = lax.broadcasted_iota(jnp.int32, (S_DEV, S_DEV), 1)
    rows = jnp.broadcast_to(rows_ref[...].astype(F32), (S_DEV, S_DEV))
    row_col = jnp.sum(jnp.where(r_i == c_i, rows, 0.0), axis=1, keepdims=True)
    tok = lax.broadcasted_iota(jnp.int32, onehot.shape, 1).astype(F32)
    onehot[...] = jnp.where(tok == row_col, 1.0, 0.0).astype(BF16)
    ss[2, 0, 0, :, :] = jnp.zeros((8, HALF), F32)

    pick_b = sems.take(16)
    pair_b = sems.take(16)
    rel_b = sems.take(4)
    rsp_b = sems.take(8)
    rows2_b = sems.take(4)
    g1_b = sems.take(4)
    g2_b = sems.take(4)
    rs2_b = sems.take(4)
    rs3_b = sems.take(1)
    rs4_b = sems.take(1)
    gx_b = sems.take(3)
    gz_b = sems.take(3)
    inv_b = sems.take(2)
    s_b = sems.take(32)
    t_b = sems.take(32)
    out_b = sems.take(1)

    def pick_copy(i, p, uu, vv, k):
        return rcopy(
            picks.at[:, p], r1.at[:, vv, k], pick_b + i, pick_b + vv * 4 + k, at(dev_uv(uu, v, c))
        )

    def pick_body(i, _):
        p = visit(i)[0]
        act_copy(i, p).wait()
        res = jnp.dot(onehot[...], act[:, columns(p)], preferred_element_type=F32).astype(BF16)
        for zz in range(2):
            picks[zz, p, :, :] = res[:, zz * BLK:(zz + 1) * BLK]
        return 0

    def pick_send(i, _):
        p, uu, vv, k = visit(i)

        @pl.when(k != 0)
        def _():
            pick_copy(i, p, uu, vv, k).start()

        @pl.when(k == 0)
        def _():
            r1[:, vv, 0, :, :] = picks[:, p, :, :]

        return 0

    with jax.named_scope("picks"):
        lax.fori_loop(0, 16, pick_body, 0)
    cot_copy.wait()
    pg[...] = jnp.dot(onehot[...], cot_ref[...], preferred_element_type=F32).astype(BF16)

    def g1_copy(k):
        return rcopy(pg, g1.at[k], g1_b + k, g1_b + k, peer_u(k))

    with jax.named_scope("barrier"):
        pl.semaphore_wait(barrier, 33)
    lax.fori_loop(0, 16, pick_send, 0)
    for k in (2, 1, 3):
        g1_copy(k).start()
    cott[...] = cot_ref[...].T

    def grad_pair(i):
        code = jnp.int32(0)
        for n, (a, b) in enumerate(GRAD_ORDER):
            code = jnp.where(i == n, a * 4 + b, code)
        return wrap(x + lax.div(code, 4)) * 4 + wrap(y + lax.rem(code, 4))

    def pair_copy(i, p):
        return rcopy(buf.at[oc, p], pairs.at[p], pair_b + i, pair_b + p, peer_c)

    def grad_part(i):
        p = grad_pair(i)
        res = jnp.dot(cott[...], act[:, columns(p)], preferred_element_type=F32)
        for h in range(2):
            for zz in range(2):
                buf[h, p, zz, :, :] = res[h * HALF:(h + 1) * HALF, zz * BLK:(zz + 1) * BLK]
        pair_copy(i, p).start()

    def pair_sum(i):
        p = grad_pair(i)
        pair_copy(i, p).wait_recv()
        buf[c, p, :, :, :] = buf[c, p, :, :, :] + pairs[p, :, :, :]

    def early(i, _):
        grad_part(i)
        return 0

    def late(i, _):
        grad_part(i)
        pair_sum(i - LAG)
        return 0

    def rest(i, _):
        pair_sum(i)
        return 0

    UP, DOWN = (2, 1), (3, 0)

    def block(k, m):
        return buf.at[c, pair_of(wrap(u + k), wrap(v + m))]

    def rel_copy(k, n):
        m = (UP if k == 1 else DOWN)[n]
        i = rel_b + (k // 2) * 2 + n
        return rcopy(block(2, m), rel.at[k // 2, n], i, i, peer_u(k))

    def rs1_copy(k, m):
        i = rsp_b + (k // 2) * 4 + m
        return rcopy(block(k, m), rs1.at[k // 2, m], i, i, peer_u(k))

    with jax.named_scope("grad_a"):
        lax.fori_loop(0, LAG, early, 0)
        lax.fori_loop(LAG, 7 + LAG, late, 0)
    for n in range(REL_EARLY):
        for k in (1, 3):
            rel_copy(k, n).start()
    with jax.named_scope("grad_b"):
        lax.fori_loop(7 + LAG, 16, late, 0)

    def g2_copy(k):
        return rcopy(g1, g2.at[k], g2_b + k, g2_b + k, peer_v(k))

    def rows2_copy(k):
        return rcopy(r1.at[:, wrap(v + k)], r2.at[:, k], rows2_b + k, rows2_b + k, peer_v(k))

    def pick_wait(vv, k):
        rcopy(picks.at[:, 0], r1.at[:, vv, k], pick_b, pick_b + vv * 4 + k, peer_u(k)).wait_recv()

    with jax.named_scope("rows1wait"):
        for k in (2, 1, 3):
            for kk in (1, 2, 3):
                pick_wait(wrap(v + k), kk)
            rows2_copy(k).start()
        for k in (2, 1, 3):
            g1_copy(k).wait_recv()
        g1[0, :, :] = pg[...]
        for k in (2, 1, 3):
            g2_copy(k).start()
        for kk in (1, 2, 3):
            pick_wait(v, kk)

    with jax.named_scope("grad_c"):
        lax.fori_loop(16 - LAG, 16, rest, 0)
    for n in range(REL_EARLY, 2):
        for k in (1, 3):
            rel_copy(k, n).start()

    def fill_table(i, _):
        b = jnp.int32(-1)
        for q in range(32):
            b = jnp.where(owner_ref[q] == i, q, b)
        table[i] = b
        return 0

    with jax.named_scope("table"):
        lax.fori_loop(0, 64, fill_table, 0)

    def gx_copy(n):
        return rcopy(gr.at[n], gx.at[n], gx_b + n, gx_b + n, peer_c)

    with jax.named_scope("rows2wait"):
        for zz in range(2):
            gr[zz, :, :] = gram(r1[zz, v, :, :, :].reshape(4 * S_DEV, BLK))
        gr[2, :, :] = gram(g1[...].reshape(4 * S_DEV, BLK))
        for k in (1, 3, 2):
            rows2_copy(k).wait_recv()
            for zz in range(2):
                gr[zz, :, :] += gram(r2[zz, k, :, :, :].reshape(4 * S_DEV, BLK))

    @pl.when(c == 1)
    def _():
        gx_copy(oz).start()
        gx_copy(z).start()

    for n in range(2):
        rs1_copy(1, DOWN[n]).start()
        rs1_copy(3, UP[n]).start()

    def gz_copy(n):
        half = pl.ds(n * HALF, HALF)
        return rcopy(gh.at[half], gz.at[half], gz_b + n, gz_b + n, peer_w if n else peer_z)

    gz_all = rcopy(gh, gz, gz_b + 2, gz_b + 2, peer_z)

    @pl.when(c == 0)
    def _():
        with jax.named_scope("gx"):
            gx_copy(oz).wait_recv()
        gh[...] = gr[oz, :, :] + gx[oz, :, :]
        gz_copy(0).start()
        gz_copy(1).start()
        gx_copy(z).wait_recv()
        m_ref[...] = gr[z, :, :] + gx[z, :, :]

    with jax.named_scope("g2wait"):
        for k in (1, 3, 2):
            g2_copy(k).wait_recv()
            gr[2, :, :] += gram(g2[k, :, :, :].reshape(4 * S_DEV, BLK))

    @pl.when(c == 0)
    def _():
        gx_copy(2).start()

    @pl.when(c == 1)
    def _():
        with jax.named_scope("gxg"):
            gx_copy(2).wait_recv()
        gh[...] = gr[2, :, :] + gx[2, :, :]
        gz_all.start()
        m_ref[...] = gh[...]

    with jax.named_scope("relay"):
        for n in range(2):
            for k in (1, 3):
                rel_copy(k, n).wait_recv()
                m = (UP if k == 1 else DOWN)[n]
                p = pair_of(wrap(u + k), wrap(v + m))
                buf[c, p, :, :, :] = buf[c, p, :, :, :] + rel[k // 2, n, :, :, :]
                rs1_copy(k, m).start()

    with jax.named_scope("gz"):
        @pl.when(c == 0)
        def _():
            gz_copy(0).wait_recv()
            gz_copy(1).wait_recv()

        @pl.when(c == 1)
        def _():
            gz_all.wait_recv()

    cf = c.astype(F32)
    scale = (1.0 - cf) / 4096.0 + cf * 12.0
    m_ref[...] = (m_ref[...] + gz[...]) * scale + DAMPING * eye(BLK)
    with jax.named_scope("newton_begin"):
        newton_begin(m_ref, x_ref, e_ref)

    def s_copy(n):
        xx, yy, zz, dz, dx, dy = chip(n)
        return rcopy(isl.at[zz, xx * 4 + yy], ss.at[dz, dx, dy], s_b + n, s_b + n, chip_dev(n))

    def s_start(n, _):
        s_copy(n).start()
        return 0

    half_copy = rcopy(isx, isl, inv_b, inv_b, peer_c)
    ginv_copy = rcopy(x_ref, ginv, inv_b + 1, inv_b + 1, peer_c)

    @pl.when(c == 0)
    def _():
        with jax.named_scope("newton_end"):
            newton_end(x_ref, e_ref)
        for zz in range(2):
            cols = pl.ds(zz * HALF, HALF)
            isx[zz, :, :, :] = x_ref[HALF:, cols].reshape(16, 8, HALF)
            isl[zz, :, :, :] = x_ref[:HALF, cols].reshape(16, 8, HALF)
        half_copy.start()
        lax.fori_loop(1, 32, s_start, 0)

    @pl.when(c == 1)
    def _():
        with jax.named_scope("half"):
            half_copy.wait_recv()
        lax.fori_loop(1, 32, s_start, 0)
        with jax.named_scope("newton_end"):
            newton_end(x_ref, e_ref)
        ginv_copy.start()

    ss[0, 0, 0, :, :] = isl[z, x * 4 + y, :, :]

    def rs2_copy(k):
        return rcopy(acc1.at[k], rs2.at[k], rs2_b + k, rs2_b + k, peer_v(k))

    with jax.named_scope("rs1"):
        for m in (3, 2, 1, 0):
            rs1_copy(1, m).wait_recv()
            rs1_copy(3, m).wait_recv()
            acc1[m, :, :, :] = block(0, m)[...] + rs1[0, m, :, :, :] + rs1[1, m, :, :, :]
            if m:
                rs2_copy(m).start()

    def s_wait(n, _):
        s_copy(n).wait_recv()
        return 0

    def t_copy(n):
        xx, yy, zz, dz, dx, dy = chip(n)
        return rcopy(dd.at[dz, dx, dy], tt.at[dz, dx, dy], t_b + n, t_b + n, chip_dev(n))

    def select(n, _):
        xx, yy, zz, dz, dx, dy = chip(n)
        for cc in range(2):
            b = table[dev(xx, yy, zz, cc)]
            bb = jnp.maximum(b, 0)
            bz = lax.rem(bb, 2)
            by = lax.rem(lax.div(bb, 2), 4)
            bx = lax.div(bb, 8)
            none = b < 0
            i0 = jnp.where(none, 2, lax.rem(bz + z, 2))
            i1 = jnp.where(none, 0, wrap(x - bx + 4))
            i2 = jnp.where(none, 0, wrap(y - by + 4))
            dd[dz, dx, dy, cc, :, :] = ss[i0, i1, i2, :, :]

        @pl.when(n > 0)
        def _():
            t_copy(n).start()

        return 0

    with jax.named_scope("s"):
        lax.fori_loop(1, 32, s_wait, 0)
    with jax.named_scope("select"):
        lax.fori_loop(0, 32, select, 0)
    tt[0, 0, 0, :, :, :] = dd[0, 0, 0, :, :, :]

    with jax.named_scope("rs2"):
        for k in (3, 2, 1):
            rs2_copy(k).wait_recv()
    acc2[...] = acc1[0, :, :, :] + rs2[1, :, :, :] + rs2[2, :, :, :] + rs2[3, :, :, :]
    rs3_copy = rcopy(acc2.at[oz], rs3, rs3_b, rs3_b, peer_z)
    rs3_copy.start()

    with jax.named_scope("rs3"):
        rs3_copy.wait_recv()
    fin[c, :, :] = acc2[z, :, :] + rs3[...]
    rs4_copy = rcopy(fin.at[c], fin.at[c], rs4_b, rs4_b, peer_c)
    rs4_copy.start()

    def t_wait(n, _):
        t_copy(n).wait_recv()
        return 0

    def assemble(n, _):
        dz, dx, dy = lax.div(n, 16), lax.rem(lax.div(n, 4), 4), lax.rem(n, 4)
        row = wrap(x - dx + 4) * 4 + wrap(y - dy + 4)
        zz = lax.rem(z + dz, 2)
        for cc in range(2):
            outh[cc, 0, zz, row, :, :] = tt[dz, dx, dy, cc, :, :]
        return 0

    with jax.named_scope("t"):
        lax.fori_loop(1, 32, t_wait, 0)
    lax.fori_loop(0, 32, assemble, 0)
    out_copy = rcopy(outh.at[oc, 0], outh.at[oc, 1], out_b, out_b, peer_c)
    out_copy.start()

    with jax.named_scope("rs4"):
        rs4_copy.wait_recv()

    @pl.when(c == 0)
    def _():
        ginv_copy.wait_recv()

    @pl.when(c == 1)
    def _():
        ginv[...] = x_ref[...]

    with jax.named_scope("final"):
        grad = fin[...].reshape(BLK, BLK)
        nt = (((1,), (1,)), ((), ()))
        left = dot_hi(isl[0, :, :, :].reshape(HALF, HALF), grad[:, :HALF], nt)
        left += dot_hi(isl[1, :, :, :].reshape(HALF, HALF), grad[:, HALF:], nt)
        step_v[...] = dot_hi(left, ginv[...])
    step_copy = pltpu.make_async_copy(step_v, step_hbm, out_sem.at[0])
    step_copy.start()

    with jax.named_scope("outx"):
        out_copy.wait_recv()
    for n in range(2):
        h = (1 - n) * c + n * oc
        for zz in range(2):
            slot_v[h, :, zz * HALF:(zz + 1) * HALF] = outh[c, n, zz, :, :, :].reshape(HALF, HALF)
    slot_copy = pltpu.make_async_copy(slot_v, slot_hbm, out_sem.at[1])
    slot_copy.start()

    def drain(i, _):
        pair_copy(i, grad_pair(i)).wait_send()
        p, uu, vv, k = visit(i)

        @pl.when(k != 0)
        def _():
            pick_copy(i, p, uu, vv, k).wait_send()

        return 0

    def drain_slots(n, _):
        s_copy(n).wait_send()
        t_copy(n).wait_send()
        return 0

    with jax.named_scope("drain"):
        lax.fori_loop(0, 16, drain, 0)
        lax.fori_loop(1, 32, drain_slots, 0)

        @pl.when(c == 0)
        def _():
            for copy in [gx_copy(2), gz_copy(0), gz_copy(1), half_copy]:
                copy.wait_send()

        @pl.when(c == 1)
        def _():
            for copy in [gx_copy(oz), gx_copy(z), gz_all, ginv_copy]:
                copy.wait_send()

        for n in range(2):
            for k in (1, 3):
                rel_copy(k, n).wait_send()
        for m in range(4):
            for k in (1, 3):
                rs1_copy(k, m).wait_send()
        for k in (1, 2, 3):
            for make in (g1_copy, g2_copy, rows2_copy, rs2_copy):
                make(k).wait_send()
        for copy in [rs3_copy, rs4_copy, out_copy]:
            copy.wait_send()
    with jax.named_scope("store"):
        step_copy.wait()
        slot_copy.wait()


def per_device(activations, cotangent, sampled_rows, block_owner):
    tokens, width = activations.shape
    vmem = pltpu.VMEM
    step, slot = pl.pallas_call(
        kernel,
        out_shape=(
            jax.ShapeDtypeStruct((HALF, BLK), F32),
            jax.ShapeDtypeStruct((2, HALF, BLK), F32),
        ),
        in_specs=[
            pl.BlockSpec(memory_space=pl.ANY),
            pl.BlockSpec(memory_space=pl.ANY),
            pl.BlockSpec(memory_space=pltpu.VMEM),
            pl.BlockSpec(memory_space=pltpu.SMEM),
        ],
        out_specs=(
            pl.BlockSpec(memory_space=pl.ANY),
            pl.BlockSpec(memory_space=pl.ANY),
        ),
        scratch_shapes=[
            vmem((tokens, width), BF16),
            vmem((tokens, BLK), BF16),
            vmem((BLK, tokens), BF16),
            vmem((S_DEV, tokens), BF16),
            vmem((2, 16, 2, HALF, BLK), F32),
            vmem((16, 2, HALF, BLK), F32),
            vmem((2, 2, 2, HALF, BLK), F32),
            vmem((2, 4, 2, HALF, BLK), F32),
            vmem((4, 2, HALF, BLK), F32),
            vmem((4, 2, HALF, BLK), F32),
            vmem((2, HALF, BLK), F32),
            vmem((HALF, BLK), F32),
            vmem((2, HALF, BLK), F32),
            vmem((2, 16, S_DEV, BLK), BF16),
            vmem((S_DEV, BLK), BF16),
            vmem((2, 4, 4, S_DEV, BLK), BF16),
            vmem((2, 4, 4, S_DEV, BLK), BF16),
            vmem((4, S_DEV, BLK), BF16),
            vmem((4, 4, S_DEV, BLK), BF16),
            vmem((3, BLK, BLK), F32),
            vmem((3, BLK, BLK), F32),
            vmem((BLK, BLK), F32),
            vmem((BLK, BLK), F32),
            vmem((BLK, BLK), F32),
            vmem((BLK, BLK), F32),
            vmem((BLK, BLK), F32),
            vmem((2, 16, 8, HALF), F32),
            vmem((2, 16, 8, HALF), F32),
            vmem((BLK, BLK), F32),
            vmem((3, 4, 4, 8, HALF), F32),
            vmem((2, 4, 4, 2, 8, HALF), F32),
            vmem((2, 4, 4, 2, 8, HALF), F32),
            vmem((2, 2, 2, 16, 8, HALF), F32),
            vmem((2, HALF, BLK), F32),
            vmem((HALF, BLK), F32),
            pltpu.SMEM((64,), jnp.int32),
            pltpu.SemaphoreType.DMA((17,)),
            pltpu.SemaphoreType.DMA((2,)),
            pltpu.SemaphoreType.DMA((SEM_TOTAL,)),
            pltpu.SemaphoreType.DMA((SEM_TOTAL,)),
        ],
        compiler_params=pltpu.CompilerParams(
            collective_id=0, has_side_effects=True, vmem_limit_bytes=60 * 1024 * 1024
        ),
    )(activations, cotangent, sampled_rows.reshape(1, S_DEV), block_owner)
    return step, slot.reshape(1, BLK, BLK)


def solution(mesh):
    return jax.shard_map(
        per_device,
        mesh=mesh,
        in_specs=(P("dp", None), P("dp", "tensor"), P("dp"), P()),
        out_specs=(P("dp", "tensor"), P("dp", None, None)),
        check_vma=False,
    )
```

time: 976 us -> 73.2 us (0.07)
  waiting for transfers between devices: 875 us -> 0 us
  Pallas kernels: 0 us -> 69.2 us
  matrix products: 44 us -> 0 us
  starting transfers between devices: 16.9 us -> 0 us
  between operations: 16.6 us -> 0.64 us
  local copies, waits for them, and re-layouts: 17.5 us -> 3.24 us
    psum x1 -> x0, waiting for transfers between devices: 438 us -> none  [per_device(): g_total = lax.psum(g_partial, 'dp')]
    reduce_scatter x1 -> x0, waiting for transfers between devices: 286 us -> none  [per_device(): lax.psum_scatter(lax.dot_general(activations, cotangent, (((0,), (0,)), (...]
    all_gather x1 -> x0, waiting for transfers between devices: 122 us -> none  [per_device(): shard_piece = lax.all_gather(owned_out, 'dp', axis=0, tiled=True)]
    pallas_call x0 -> x1, Pallas kernels: none -> 69.2 us  [per_device(): pl.pallas_call(kernel, out_shape=(jax.ShapeDtypeStruct((HALF, BLK), F32),...]
    dot_general x47 -> x0, matrix products: 44 us -> none  [the longest x20 11.9 us: advance(): jnp.einsum('nij,njk->nik', current, 2.0 * identity[None, :, :] - product,...]
    all_to_all x1 -> x0, waiting for transfers between devices: 29 us -> none  [per_device(): lax.all_to_all(outgoing, 'dp', split_axis=0, concat_axis=0, tiled=True)]
    all_to_all x1 -> x0, starting transfers between devices: 10.3 us -> none  [per_device(): lax.all_to_all(outgoing, 'dp', split_axis=0, concat_axis=0, tiled=True)]
  transfers between devices with their start and end apart: 5 -> 0, of which waited for: 4 -> 0; matrix products, arithmetic and copies ran while one was open for 6% -> 0% of each run, Pallas kernels for 0% -> 0%
where the time goes in v2:
time: 73.2 us; the launch traced here: 73.1 us
  Pallas kernels  69.2 us (95%)
  local copies, waits for them, and re-layouts  3.24 us (4%)
    pallas_call x1, Pallas kernels, per_device(): pl.pallas_call(kernel, out_shape=(jax.ShapeDtypeStruct((HALF, BLK), F32),...  69.2 us
    unnamed x2, local copies, waits for them, and re-layouts  3.24 us

profile of v2, /device:TPU:1, one launch (start us, length us, event | category | flops | bytes accessed | tf_op | source)
XLA Modules:
  0.0 73.1 jit_solution(17528836447912542152)
XLA Ops:
  0.6 69.2 %shard_map.59 = (f32[128,256]{1,0:T(8,128)}, f32[2,128,256]{2,1,0:T(8,128)}) custom-call(bf16[768,8192]{1,0:T(8,128)(2,1)} %act_hbm.1, bf16[768,256]{1,0:T(8,128)(2,1)} %cot_hbm.1, s32[1,64]{1,0:T(1,128)} %bitcast.3, s32[32]{0:T(128)} %owner_ref.1), custom_call_target="tpu_custom_call" | custom-call | tf_op jit(solution)/shard_map/pallas_call | solution.py:602
  69.8 1.6 %copy.8 = f32[128,256]{1,0:T(8,128)} copy(f32[128,256]{1,0:T(8,128)} %get-tuple-element.8) | data formatting | bytes 262144
  71.4 1.7 %copy.9 = f32[1,256,256]{2,1,0:T(8,128)} copy(f32[1,256,256]{2,1,0:T(8,128)} %bitcast.2) | data formatting | bytes 524288

commit v3 on v2

v3 whole, which is shorter than its diff:
```python
import jax
import jax.numpy as jnp
from jax import lax
from jax.experimental import pallas as pl
from jax.experimental.pallas import tpu as pltpu
from jax.sharding import PartitionSpec as P

S_DEV = 64
BLK = 256
HALF = 128
ITERS = 10
DAMPING = 0.05
MESH = pl.DeviceIdType.MESH
HI = lax.Precision.HIGHEST
F32 = jnp.float32
BF16 = jnp.bfloat16


class Sems:
    def __init__(self):
        self.used = 0

    def __call__(self, count=1):
        base = self.used
        self.used += count
        return base


SENDS = 24
RECVS = 64
LAG = 3
GRAD_SPLIT = 11
PICKS_FIRST = 8
TAIL = 32
MAIN = HALF - TAIL
SENT = BLK - TAIL
GRAD_ORDER = (
    (2, 2), (2, 1), (1, 2), (2, 3), (3, 2), (2, 0), (0, 2),
    (1, 1), (1, 3), (3, 1), (3, 3), (1, 0), (0, 1), (3, 0), (0, 3), (0, 0),
)


def dot_hi(a, b, dims=(((1,), (0,)), ((), ()))):
    return lax.dot_general(a, b, dims, precision=HI, preferred_element_type=F32)


def gram(rows):
    return lax.dot_general(rows, rows, (((0,), (0,)), ((), ())), preferred_element_type=F32)


def eye(n):
    r = lax.broadcasted_iota(jnp.int32, (n, n), 0)
    c = lax.broadcasted_iota(jnp.int32, (n, n), 1)
    return jnp.where(r == c, 1.0, 0.0).astype(F32)


def newton_step(x_ref, e_ref):
    def step(k, _):
        e = e_ref[...]
        x = x_ref[...]
        both = dot_hi(jnp.concatenate([x, e], axis=0), e)
        x_ref[...] = x + both[:BLK]
        e_ref[...] = both[BLK:]
        return 0

    return step


def newton_begin(m_ref, x_ref, e_ref):
    ident = eye(BLK)
    m = m_ref[...]
    bound = jnp.max(jnp.sum(jnp.abs(m), axis=1, keepdims=True), axis=0, keepdims=True)
    inv = 1.0 / bound
    e = ident - m * inv
    x_ref[...] = (ident + e) * inv
    e_ref[...] = dot_hi(e, e)
    lax.fori_loop(0, 4, newton_step(x_ref, e_ref), 0)
    e_ref[...] = ident - dot_hi(m, x_ref[...])


def newton_end(x_ref, e_ref):
    lax.fori_loop(0, 4, newton_step(x_ref, e_ref), 0)
    x_ref[...] += dot_hi(x_ref[...], e_ref[...])


def kernel(
    act_hbm, cot_hbm, rows_ref, owner_ref,
    step_hbm, slot_hbm,
    act, cot_ref, cott, onehot, buf, pairs, zb, rel, rs1, acc1, rs2a, rs2b, acc2, rs3, fin,
    picks, pg, r1, r2, g1, g2,
    gr, gx, gh, gz, m_ref, x_ref, e_ref, isl, isx, ginv,
    ss, dd, tt, outh, slot_v, step_v, table,
    act_sem, out_sem, send_sem, recv_sem,
):
    dp = lax.axis_index("dp")
    ten = lax.axis_index("tensor")
    c = lax.rem(dp, 2)
    z = lax.rem(lax.div(dp, 2), 2)
    y = lax.rem(lax.div(dp, 4), 4)
    x = lax.div(dp, 16)
    u = (1 - c) * x + c * y
    v = (1 - c) * y + c * x
    oc = 1 - c
    oz = 1 - z

    def wrap(a):
        return lax.rem(a, 4)

    def dev(xx, yy, zz, cc):
        return ((xx * 4 + yy) * 2 + zz) * 2 + cc

    def dev_uv(uu, vv, cc):
        return dev((1 - c) * uu + c * vv, (1 - c) * vv + c * uu, z, cc)

    def at(d):
        return {"dp": d, "tensor": ten}

    def peer_u(k):
        return at(dev_uv(wrap(u + k), v, c))

    def peer_v(k):
        return at(dev_uv(u, wrap(v + k), c))

    peer_z = at(dev(x, y, oz, c))
    peer_w = {"dp": dev(x, y, oz, c), "tensor": wrap(ten + 3 + 2 * z)}
    peer_c = at(dev(x, y, z, oc))

    def pair_of(uu, vv):
        return (1 - c) * (uu * 4 + vv) + c * (vv * 4 + uu)

    sends, recvs = Sems(), Sems()

    def rcopy(src, dst, send_i, recv_i, to):
        return pltpu.make_async_remote_copy(
            src_ref=src, dst_ref=dst, send_sem=send_sem.at[send_i], recv_sem=recv_sem.at[recv_i],
            device_id=to, device_id_type=MESH,
        )

    def wait_sent(ref, send_i):
        rcopy(ref, ref, send_i, 0, peer_c).wait_send()

    def wait_got(ref, recv_i):
        rcopy(ref, ref, 0, recv_i, peer_c).wait_recv()

    def columns(p):
        return pl.ds(pl.multiple_of(p * 2 * BLK, 2 * BLK), 2 * BLK)

    def act_copy(i, p):
        return pltpu.make_async_copy(act_hbm.at[:, columns(p)], act.at[:, columns(p)], act_sem.at[i])

    def visit(i):
        g = wrap(x + wrap(lax.div(i, 4) + 1))
        j = wrap(y + wrap(lax.rem(i, 4) + 1))
        uu = (1 - c) * g + c * j
        vv = (1 - c) * j + c * g
        return g * 4 + j, uu, vv, wrap(uu - u + 4)

    def start_load(i, _):
        act_copy(i, visit(i)[0]).start()
        return 0

    barrier = pltpu.get_barrier_semaphore()

    def chip(n):
        dz, dx, dy = lax.div(n, 16), lax.rem(lax.div(n, 4), 4), lax.rem(n, 4)
        xx, yy, zz = wrap(x + dx), wrap(y + dy), lax.rem(z + dz, 2)
        return xx, yy, zz, dz, dx, dy

    def chip_dev(n):
        xx, yy, zz, dz, dx, dy = chip(n)
        other = dz * lax.rem(dx + dy, 2)
        return {"dp": dev(xx, yy, zz, c), "tensor": wrap(ten + other * (3 + 2 * z))}

    def greet(n, _):
        pl.semaphore_signal(barrier, inc=1, device_id=chip_dev(32 - n), device_id_type=MESH)
        return 0

    lax.fori_loop(1, 32, greet, 0)
    for to in [peer_w, peer_c]:
        pl.semaphore_signal(barrier, inc=1, device_id=to, device_id_type=MESH)
    lax.fori_loop(0, 16, start_load, 0)
    cot_copy = pltpu.make_async_copy(cot_hbm, cot_ref, act_sem.at[16])
    cot_copy.start()


    r_i = lax.broadcasted_iota(jnp.int32, (S_DEV, S_DEV), 0)
    c_i = lax.broadcasted_iota(jnp.int32, (S_DEV, S_DEV), 1)
    rows = jnp.broadcast_to(rows_ref[...].astype(F32), (S_DEV, S_DEV))
    row_col = jnp.sum(jnp.where(r_i == c_i, rows, 0.0), axis=1, keepdims=True)
    tok = lax.broadcasted_iota(jnp.int32, onehot.shape, 1).astype(F32)
    onehot[...] = jnp.where(tok == row_col, 1.0, 0.0).astype(BF16)
    ss[32, :, :] = jnp.zeros((8, HALF), F32)

    pick_s, pick_r = sends(), recvs(4)
    pair_s, pair_r = sends(), recvs(16)
    zb_s, zb_r = sends(), recvs(2)
    rel_s, rel_r = sends(), recvs(4)
    rs1_s, rs1_r = sends(), recvs(8)
    rows2_s, rows2_r = sends(), recvs(4)
    g1_s, g1_r = sends(), recvs()
    g2_s, g2_r = sends(), recvs(4)
    rs2_s, rs2_r = sends(2), recvs(2)
    rs3_s, rs3_r = sends(), recvs()
    rs4_s, rs4_r = sends(), recvs()
    gx_s, gx_r = sends(3), recvs(3)
    gz_s, gz_r = sends(3), recvs(3)
    inv_s, inv_r = sends(2), recvs(2)
    s_s, s_r = sends(), recvs()
    t_s, t_r = sends(), recvs()
    out_s, out_r = sends(), recvs()
    assert sends.used <= SENDS and recvs.used <= RECVS

    def pick_copy(p, uu, vv, k):
        return rcopy(
            picks.at[:, p], r1.at[:, vv, k], pick_s, pick_r + vv, at(dev_uv(uu, v, c))
        )

    def pick_body(i, _):
        p = visit(i)[0]
        act_copy(i, p).wait()
        res = jnp.dot(onehot[...], act[:, columns(p)], preferred_element_type=F32).astype(BF16)
        for zz in range(2):
            picks[zz, p, :, :] = res[:, zz * BLK:(zz + 1) * BLK]
        return 0

    def pick_send(i, _):
        p, uu, vv, k = visit(i)

        @pl.when(k != 0)
        def _():
            pick_copy(p, uu, vv, k).start()

        @pl.when(k == 0)
        def _():
            r1[:, vv, 0, :, :] = picks[:, p, :, :]

        return 0

    def pick_both(i, _):
        pick_body(i, 0)
        return pick_send(i, 0)

    with jax.named_scope("picks"):
        lax.fori_loop(0, PICKS_FIRST, pick_body, 0)
    with jax.named_scope("barrier"):
        pl.semaphore_wait(barrier, 33)
    with jax.named_scope("picks2"):
        lax.fori_loop(0, PICKS_FIRST, pick_send, 0)
        lax.fori_loop(PICKS_FIRST, 16, pick_both, 0)
    cot_copy.wait()
    pg[...] = jnp.dot(onehot[...], cot_ref[...], preferred_element_type=F32).astype(BF16)

    def g1_copy(k):
        return rcopy(pg, g1.at[k], g1_s, g1_r, peer_u(k))

    for k in (2, 1, 3):
        g1_copy(k).start()
    cott[...] = cot_ref[...].T

    def grad_pair(i):
        code = jnp.int32(0)
        for n, (a, b) in enumerate(GRAD_ORDER):
            code = jnp.where(i == n, a * 4 + b, code)
        return wrap(x + lax.div(code, 4)) * 4 + wrap(y + lax.rem(code, 4))

    def pair_copy(i, p):
        return rcopy(buf.at[oc, p], pairs.at[p], pair_s, pair_r + i, peer_c)

    def grad_part(i):
        p = grad_pair(i)
        res = jnp.dot(cott[...], act[:, columns(p)], preferred_element_type=F32)
        for zz in range(2):
            other = lax.rem(zz + z, 2)
            main = pl.ds(pl.multiple_of(MAIN - MAIN * other, 8), MAIN)
            tail = pl.ds(pl.multiple_of(2 * MAIN + TAIL * other, 8), TAIL)
            for h in range(2):
                part = res[h * HALF:(h + 1) * HALF, zz * BLK:(zz + 1) * BLK]
                buf[h, p, main, :] = part[:MAIN]
                buf[h, p, tail, :] = part[MAIN:]
        pair_copy(i, p).start()

    def zb_copy(i, p, group):
        return rcopy(buf.at[c, p, SENT:], zb.at[i], zb_s, zb_r + group, peer_z)

    def pair_sum(i):
        p = grad_pair(i)
        pair_copy(i, p).wait_recv()
        buf[c, p, :, :] = buf[c, p, :, :] + pairs[p, :, :]
        @pl.when(i < 7)
        def _():
            zb_copy(i, p, 0).start()

        @pl.when(i >= 7)
        def _():
            zb_copy(i, p, 1).start()

    def early(i, _):
        grad_part(i)
        return 0

    def late(i, _):
        grad_part(i)
        pair_sum(i - LAG)
        return 0

    def rest(i, _):
        pair_sum(i)
        return 0

    def zb_add(i, _):
        p = grad_pair(i)
        buf[c, p, SENT - TAIL:SENT, :] = buf[c, p, SENT - TAIL:SENT, :] + zb[i, :, :]
        return 0

    UP, DOWN = (2, 1), (3, 0)

    def block(k, m):
        return buf.at[c, pair_of(wrap(u + k), wrap(v + m)), 0:SENT]

    def rel_copy(k, n):
        m = (UP if k == 1 else DOWN)[n]
        return rcopy(block(2, m), rel.at[k // 2, n], rel_s, rel_r + (k // 2) * 2 + n, peer_u(k))

    def rs1_copy(k, m):
        return rcopy(block(k, m), rs1.at[k // 2, m], rs1_s, rs1_r + (k // 2) * 4 + m, peer_u(k))

    with jax.named_scope("grad_a"):
        lax.fori_loop(0, LAG, early, 0)
        lax.fori_loop(LAG, GRAD_SPLIT, late, 0)

    def g2_copy(k):
        return rcopy(g1, g2.at[k], g2_s, g2_r + k, peer_v(k))

    def rows2_copy(k):
        return rcopy(r1.at[:, wrap(v + k)], r2.at[:, k], rows2_s, rows2_r + k, peer_v(k))

    with jax.named_scope("rows1wait"):
        for k in (2, 1, 3):
            wait_got(r1.at[:, wrap(v + k), 1:4], pick_r + wrap(v + k))
            rows2_copy(k).start()
        wait_got(g1.at[1:4], g1_r)
        g1[0, :, :] = pg[...]
        for k in (2, 1, 3):
            g2_copy(k).start()
        wait_got(r1.at[:, v, 1:4], pick_r + v)

    with jax.named_scope("grad_b"):
        lax.fori_loop(GRAD_SPLIT, 16, late, 0)
    with jax.named_scope("grad_c"):
        lax.fori_loop(16 - LAG, 16, rest, 0)
        wait_got(zb.at[0:7], zb_r)
        lax.fori_loop(0, 7, zb_add, 0)
    for n in range(2):
        for k in (1, 3):
            rel_copy(k, n).start()

    def fill_table(i, _):
        xx, yy, zz, _, _, _ = chip(lax.div(i, 2))
        d = dev(xx, yy, zz, lax.rem(i, 2))
        b = jnp.int32(-1)
        for q in range(32):
            b = jnp.where(owner_ref[q] == d, q, b)
        bb = jnp.maximum(b, 0)
        bz = lax.rem(bb + z, 2)
        by = wrap(y - lax.rem(lax.div(bb, 2), 4) + 4)
        bx = wrap(x - lax.div(bb, 8) + 4)
        table[i] = jnp.where(b < 0, 32, bz * 16 + bx * 4 + by)
        return 0

    with jax.named_scope("table"):
        lax.fori_loop(0, 64, fill_table, 0)

    def gx_copy(n):
        return rcopy(gr.at[n], gx.at[n], gx_s + n, gx_r + n, peer_c)

    with jax.named_scope("rows2wait"):
        for zz in range(2):
            gr[zz, :, :] = gram(r1[zz, v, :, :, :].reshape(4 * S_DEV, BLK))
        gr[2, :, :] = gram(g1[...].reshape(4 * S_DEV, BLK))
        for k in (1, 3, 2):
            rows2_copy(k).wait_recv()
            for zz in range(2):
                gr[zz, :, :] += gram(r2[zz, k, :, :, :].reshape(4 * S_DEV, BLK))

    @pl.when(c == 1)
    def _():
        gx_copy(oz).start()
        gx_copy(z).start()

    wait_got(zb.at[7:16], zb_r + 1)
    lax.fori_loop(7, 16, zb_add, 0)
    for n in range(2):
        rs1_copy(1, DOWN[n]).start()
        rs1_copy(3, UP[n]).start()

    def gz_copy(n):
        half = pl.ds(n * HALF, HALF)
        return rcopy(gh.at[half], gz.at[half], gz_s + n, gz_r + n, peer_w if n else peer_z)

    gz_all = rcopy(gh, gz, gz_s + 2, gz_r + 2, peer_z)

    @pl.when(c == 0)
    def _():
        with jax.named_scope("gx"):
            gx_copy(oz).wait_recv()
        gh[...] = gr[oz, :, :] + gx[oz, :, :]
        gz_copy(0).start()
        gz_copy(1).start()
        gx_copy(z).wait_recv()
        m_ref[...] = gr[z, :, :] + gx[z, :, :]

    with jax.named_scope("relay"):
        for n in range(2):
            for k in (1, 3):
                rel_copy(k, n).wait_recv()
                m = (UP if k == 1 else DOWN)[n]
                p = pair_of(wrap(u + k), wrap(v + m))
                buf[c, p, 0:SENT, :] = buf[c, p, 0:SENT, :] + rel[k // 2, n, :, :]
                rs1_copy(k, m).start()

    with jax.named_scope("g2wait"):
        for k in (1, 3, 2):
            g2_copy(k).wait_recv()
            gr[2, :, :] += gram(g2[k, :, :, :].reshape(4 * S_DEV, BLK))

    @pl.when(c == 0)
    def _():
        gx_copy(2).start()

    @pl.when(c == 1)
    def _():
        with jax.named_scope("gxg"):
            gx_copy(2).wait_recv()
        gh[...] = gr[2, :, :] + gx[2, :, :]
        gz_all.start()
        m_ref[...] = gh[...]

    def factor(scale):
        m_ref[...] = (m_ref[...] + gz[...]) * scale + DAMPING * eye(BLK)

    def core1_factor():
        with jax.named_scope("gz"):
            gz_all.wait_recv()
        factor(12.0)

    def s_copy(n):
        xx, yy, zz, dz, dx, dy = chip(n)
        return rcopy(isl.at[zz, xx * 4 + yy], ss.at[n], s_s, s_r, chip_dev(n))

    def s_start(n, _):
        s_copy(n).start()
        return 0

    def rs2_copy(k, part):
        rows = pl.ds(MAIN, HALF) if part else pl.ds(0, MAIN)
        to = rs2b if part else rs2a
        return rcopy(acc1.at[k, rows], to.at[k], rs2_s + part, rs2_r + part, peer_v(k))

    def rs1_finish():
        with jax.named_scope("rs1"):
            for m in (3, 2, 1, 0):
                wait_got(rs1.at[0, m], rs1_r + m)
                wait_got(rs1.at[1, m], rs1_r + 4 + m)
                acc1[m, :, :] = block(0, m)[...] + rs1[0, m, :, :] + rs1[1, m, :, :]
                if m:
                    rs2_copy(m, 0).start()
            for m in (3, 2, 1):
                rs2_copy(m, 1).start()

    half_copy = rcopy(isx, isl, inv_s, inv_r, peer_c)
    ginv_copy = rcopy(x_ref, ginv, inv_s + 1, inv_r + 1, peer_c)

    def t_copy(n):
        return rcopy(dd.at[n], tt.at[n], t_s, t_r, chip_dev(n))

    def t_start(n, _):
        t_copy(n).start()
        return 0

    def slots_back():
        ss[0, :, :] = isl[z, x * 4 + y, :, :]
        with jax.named_scope("s"):
            wait_got(ss.at[1:32], s_r)
        with jax.named_scope("select"):
            for n in range(32):
                for cc in range(2):
                    dd[n, cc, :, :] = ss[table[2 * n + cc], :, :]
            lax.fori_loop(1, 32, t_start, 0)
        tt[0, :, :, :] = dd[0, :, :, :]

    @pl.when(c == 0)
    def _():
        with jax.named_scope("gz"):
            gz_copy(0).wait_recv()
            gz_copy(1).wait_recv()
        factor(1.0 / 4096.0)
        with jax.named_scope("newton_begin"):
            newton_begin(m_ref, x_ref, e_ref)
        with jax.named_scope("newton_end"):
            newton_end(x_ref, e_ref)
        for zz in range(2):
            cols = pl.ds(zz * HALF, HALF)
            isx[zz, :, :, :] = x_ref[HALF:, cols].reshape(16, 8, HALF)
            isl[zz, :, :, :] = x_ref[:HALF, cols].reshape(16, 8, HALF)
        half_copy.start()
        lax.fori_loop(1, 32, s_start, 0)
        rs1_finish()
        slots_back()

    @pl.when(c == 1)
    def _():
        with jax.named_scope("half"):
            half_copy.wait_recv()
        lax.fori_loop(1, 32, s_start, 0)
        rs1_finish()
        core1_factor()
        with jax.named_scope("newton_begin"):
            newton_begin(m_ref, x_ref, e_ref)
        slots_back()
        with jax.named_scope("newton_end"):
            newton_end(x_ref, e_ref)
        ginv_copy.start()

    with jax.named_scope("drain"):
        wait_sent(picks.at[:, 0:12], pick_s)
        wait_sent(buf.at[oc], pair_s)
        wait_sent(zb, zb_s)
        wait_sent(g1.at[1:4], g1_s)
        wait_sent(g2.at[1:4], g2_s)
        wait_sent(r2.at[:, 1:4], rows2_s)
        wait_sent(rel, rel_s)
        wait_sent(rs1, rs1_s)

        @pl.when(c == 0)
        def _():
            for copy in [gx_copy(2), gz_copy(0), gz_copy(1), half_copy]:
                copy.wait_send()

        @pl.when(c == 1)
        def _():
            for copy in [gx_copy(oz), gx_copy(z), gz_all, ginv_copy]:
                copy.wait_send()

    with jax.named_scope("rs2a"):
        wait_got(rs2a.at[1:4], rs2_r)
    acc2[...] = acc1[0, 0:MAIN, :] + rs2a[1, :, :] + rs2a[2, :, :] + rs2a[3, :, :]
    rs3_copy = rcopy(acc2, rs3, rs3_s, rs3_r, peer_z)
    rs3_copy.start()
    with jax.named_scope("rs2b"):
        wait_got(rs2b.at[1:4], rs2_r + 1)
    fin[c, :, :] = acc1[0, MAIN:SENT, :] + rs2b[1, :, :] + rs2b[2, :, :] + rs2b[3, :, :]
    with jax.named_scope("rs3"):
        rs3_copy.wait_recv()
    fin[c, 0:MAIN, :] = fin[c, 0:MAIN, :] + rs3[...]
    rs4_copy = rcopy(fin.at[c], fin.at[c], rs4_s, rs4_r, peer_c)
    rs4_copy.start()

    def assemble(n, _):
        dz, dx, dy = lax.div(n, 16), lax.rem(lax.div(n, 4), 4), lax.rem(n, 4)
        row = wrap(x - dx + 4) * 4 + wrap(y - dy + 4)
        zz = lax.rem(z + dz, 2)
        for cc in range(2):
            outh[cc, 0, zz, row, :, :] = tt[n, cc, :, :]
        return 0

    with jax.named_scope("t"):
        wait_got(tt.at[1:32], t_r)
    lax.fori_loop(0, 32, assemble, 0, unroll=4)
    out_copy = rcopy(outh.at[oc, 0], outh.at[oc, 1], out_s, out_r, peer_c)
    out_copy.start()

    with jax.named_scope("rs4"):
        rs4_copy.wait_recv()

    @pl.when(c == 0)
    def _():
        ginv_copy.wait_recv()

    @pl.when(c == 1)
    def _():
        ginv[...] = x_ref[...]

    with jax.named_scope("final"):
        grad = fin[...].reshape(BLK, BLK)
        nt = (((1,), (1,)), ((), ()))
        left = dot_hi(isl[0, :, :, :].reshape(HALF, HALF), grad[:, :HALF], nt)
        left += dot_hi(isl[1, :, :, :].reshape(HALF, HALF), grad[:, HALF:], nt)
        step_v[...] = dot_hi(left, ginv[...])
    step_copy = pltpu.make_async_copy(step_v, step_hbm, out_sem.at[0])
    step_copy.start()

    with jax.named_scope("outx"):
        out_copy.wait_recv()
    for n in range(2):
        h = (1 - n) * c + n * oc
        for zz in range(2):
            slot_v[h, :, zz * HALF:(zz + 1) * HALF] = outh[c, n, zz, :, :, :].reshape(HALF, HALF)
    slot_copy = pltpu.make_async_copy(slot_v, slot_hbm, out_sem.at[1])
    slot_copy.start()

    with jax.named_scope("drain2"):
        wait_sent(ss.at[1:32], s_s)
        wait_sent(tt.at[1:32], t_s)
        wait_sent(rs2a.at[1:4], rs2_s)
        wait_sent(rs2b.at[1:4], rs2_s + 1)
        for copy in [rs3_copy, rs4_copy, out_copy]:
            copy.wait_send()
    with jax.named_scope("store"):
        step_copy.wait()
        slot_copy.wait()


def settle(step_in, slot_in, step_out, slot_out):
    step_out[...] = step_in[...]
    slot_out[...] = slot_in[...]


def per_device(activations, cotangent, sampled_rows, block_owner):
    tokens, width = activations.shape
    vmem = pltpu.VMEM
    step, slot = pl.pallas_call(
        kernel,
        out_shape=(
            jax.ShapeDtypeStruct((HALF, BLK), F32),
            jax.ShapeDtypeStruct((2, HALF, BLK), F32),
        ),
        in_specs=[
            pl.BlockSpec(memory_space=pl.ANY),
            pl.BlockSpec(memory_space=pl.ANY),
            pl.BlockSpec(memory_space=pltpu.VMEM),
            pl.BlockSpec(memory_space=pltpu.SMEM),
        ],
        out_specs=(
            pl.BlockSpec(memory_space=pl.ANY),
            pl.BlockSpec(memory_space=pl.ANY),
        ),
        scratch_shapes=[
            vmem((tokens, width), BF16),
            vmem((tokens, BLK), BF16),
            vmem((BLK, tokens), BF16),
            vmem((S_DEV, tokens), BF16),
            vmem((2, 16, BLK, BLK), F32),
            vmem((16, BLK, BLK), F32),
            vmem((16, TAIL, BLK), F32),
            vmem((2, 2, SENT, BLK), F32),
            vmem((2, 4, SENT, BLK), F32),
            vmem((4, SENT, BLK), F32),
            vmem((4, MAIN, BLK), F32),
            vmem((4, HALF, BLK), F32),
            vmem((MAIN, BLK), F32),
            vmem((MAIN, BLK), F32),
            vmem((2, HALF, BLK), F32),
            vmem((2, 16, S_DEV, BLK), BF16),
            vmem((S_DEV, BLK), BF16),
            vmem((2, 4, 4, S_DEV, BLK), BF16),
            vmem((2, 4, 4, S_DEV, BLK), BF16),
            vmem((4, S_DEV, BLK), BF16),
            vmem((4, 4, S_DEV, BLK), BF16),
            vmem((3, BLK, BLK), F32),
            vmem((3, BLK, BLK), F32),
            vmem((BLK, BLK), F32),
            vmem((BLK, BLK), F32),
            vmem((BLK, BLK), F32),
            vmem((BLK, BLK), F32),
            vmem((BLK, BLK), F32),
            vmem((2, 16, 8, HALF), F32),
            vmem((2, 16, 8, HALF), F32),
            vmem((BLK, BLK), F32),
            vmem((33, 8, HALF), F32),
            vmem((32, 2, 8, HALF), F32),
            vmem((32, 2, 8, HALF), F32),
            vmem((2, 2, 2, 16, 8, HALF), F32),
            vmem((2, HALF, BLK), F32),
            vmem((HALF, BLK), F32),
            pltpu.SMEM((64,), jnp.int32),
            pltpu.SemaphoreType.DMA((17,)),
            pltpu.SemaphoreType.DMA((2,)),
            pltpu.SemaphoreType.DMA((SENDS,)),
            pltpu.SemaphoreType.DMA((RECVS,)),
        ],
        compiler_params=pltpu.CompilerParams(
            collective_id=0, has_side_effects=True, vmem_limit_bytes=60 * 1024 * 1024
        ),
    )(activations, cotangent, sampled_rows.reshape(1, S_DEV), block_owner)
    step, slot = pl.pallas_call(
        settle,
        out_shape=(
            jax.ShapeDtypeStruct((HALF, BLK), F32),
            jax.ShapeDtypeStruct((2, HALF, BLK), F32),
        ),
    )(step, slot)
    return step, slot.reshape(1, BLK, BLK)


def solution(mesh):
    return jax.shard_map(
        per_device,
        mesh=mesh,
        in_specs=(P("dp", None), P("dp", "tensor"), P("dp"), P()),
        out_specs=(P("dp", "tensor"), P("dp", None, None)),
        check_vma=False,
    )
```

time: 73.2 us -> 62.8 us (0.86)
  Pallas kernels: 69.2 us -> 62 us
  local copies, waits for them, and re-layouts: 3.24 us -> 0 us
    pallas_call x1, Pallas kernels: 69.2 us -> 60.2 us  [per_device(): pl.pallas_call(kernel, out_shape=(jax.ShapeDtypeStruct((HALF, BLK), F32),...]
    unnamed x2 -> x0, local copies, waits for them, and re-layouts: 3.24 us -> none
    pallas_call x0 -> x1, Pallas kernels: none -> 1.78 us  [per_device(): pl.pallas_call(settle, out_shape=(jax.ShapeDtypeStruct((HALF, BLK), F32),...]
where the time goes in v3:
time: 62.8 us; the launch traced here: 62.7 us
  Pallas kernels  62 us (99%)
  between operations  0.64 us (1%)
    pallas_call x1, Pallas kernels, per_device(): pl.pallas_call(kernel, out_shape=(jax.ShapeDtypeStruct((HALF, BLK), F32),...  60.2 us
    pallas_call x1, Pallas kernels, per_device(): pl.pallas_call(settle, out_shape=(jax.ShapeDtypeStruct((HALF, BLK), F32),...  1.78 us

profile of v3, /device:TPU:1, one launch (start us, length us, event | category | flops | bytes accessed | tf_op | source)
XLA Modules:
  0.0 62.7 jit_solution(15420237152202349447)
XLA Ops:
  0.6 60.2 %shard_map.59 = (f32[128,256]{1,0:T(8,128)}, f32[2,128,256]{2,1,0:T(8,128)}) custom-call(bf16[768,8192]{1,0:T(8,128)(2,1)} %act_hbm.1, bf16[768,256]{1,0:T(8,128)(2,1)} %cot_hbm.1, s32[1,64]{1,0:T(1,128)} %bitcast.2, s32[32]{0:T(128)} %owner_ref.1), custom_call_target="tpu_custom_call" | custom-call | tf_op jit(solution)/shard_map/pallas_call | solution.py:621
  60.9 1.8 %shard_map.60 = (f32[128,256]{1,0:T(8,128)}, f32[2,128,256]{2,1,0:T(8,128)}) custom-call(f32[128,256]{1,0:T(8,128)} %get-tuple-element.6.step_in, f32[2,128,256]{2,1,0:T(8,128)} %get-tuple-element.7.slot_in), custom_call_target="tpu_custom_call" | custom-call | tf_op jit(solution)/shard_map/pallas_call | solution.py:685

commit v4 on v3

--- a/solution.py
+++ b/solution.py
@@ -29,6 +29,7 @@
 SENDS = 24
 RECVS = 64
 LAG = 3
+LOADS_FIRST = 3
 GRAD_SPLIT = 11
 PICKS_FIRST = 8
 TAIL = 32
@@ -159,26 +160,27 @@
         act_copy(i, visit(i)[0]).start()
         return 0
 
+    lax.fori_loop(0, LOADS_FIRST, start_load, 0)
     barrier = pltpu.get_barrier_semaphore()
 
     def chip(n):
-        dz, dx, dy = lax.div(n, 16), lax.rem(lax.div(n, 4), 4), lax.rem(n, 4)
+        if isinstance(n, int):
+            dz, dx, dy = n // 16, n // 4 % 4, n % 4
+        else:
+            dz, dx, dy = lax.div(n, 16), lax.rem(lax.div(n, 4), 4), lax.rem(n, 4)
         xx, yy, zz = wrap(x + dx), wrap(y + dy), lax.rem(z + dz, 2)
         return xx, yy, zz, dz, dx, dy
 
     def chip_dev(n):
         xx, yy, zz, dz, dx, dy = chip(n)
-        other = dz * lax.rem(dx + dy, 2)
+        other = dz * ((dx + dy) % 2)
         return {"dp": dev(xx, yy, zz, c), "tensor": wrap(ten + other * (3 + 2 * z))}
 
-    def greet(n, _):
-        pl.semaphore_signal(barrier, inc=1, device_id=chip_dev(32 - n), device_id_type=MESH)
-        return 0
-
-    lax.fori_loop(1, 32, greet, 0)
+    for n in range(31, 0, -1):
+        pl.semaphore_signal(barrier, inc=1, device_id=chip_dev(n), device_id_type=MESH)
     for to in [peer_w, peer_c]:
         pl.semaphore_signal(barrier, inc=1, device_id=to, device_id_type=MESH)
-    lax.fori_loop(0, 16, start_load, 0)
+    lax.fori_loop(LOADS_FIRST, 16, start_load, 0)
     cot_copy = pltpu.make_async_copy(cot_hbm, cot_ref, act_sem.at[16])
     cot_copy.start()
 
@@ -354,6 +356,45 @@
         for k in (1, 3):
             rel_copy(k, n).start()
 
+    def gx_copy(n):
+        return rcopy(gr.at[n], gx.at[n], gx_s + n, gx_r + n, peer_c)
+
+    with jax.named_scope("rows2wait"):
+        for zz in range(2):
+            gr[zz, :, :] = gram(r1[zz, v, :, :, :].reshape(4 * S_DEV, BLK))
+        gr[2, :, :] = gram(g1[...].reshape(4 * S_DEV, BLK))
+        for k in (1, 3, 2):
+            rows2_copy(k).wait_recv()
+            for zz in range(2):
+                gr[zz, :, :] += gram(r2[zz, k, :, :, :].reshape(4 * S_DEV, BLK))
+
+    @pl.when(c == 1)
+    def _():
+        gx_copy(oz).start()
+        gx_copy(z).start()
+
+    wait_got(zb.at[7:16], zb_r + 1)
+    lax.fori_loop(7, 16, zb_add, 0)
+    for n in range(2):
+        rs1_copy(1, DOWN[n]).start()
+        rs1_copy(3, UP[n]).start()
+
+    def gz_copy(n):
+        half = pl.ds(n * HALF, HALF)
+        return rcopy(gh.at[half], gz.at[half], gz_s + n, gz_r + n, peer_w if n else peer_z)
+
+    gz_all = rcopy(gh, gz, gz_s + 2, gz_r + 2, peer_z)
+
+    @pl.when(c == 0)
+    def _():
+        with jax.named_scope("gx"):
+            gx_copy(oz).wait_recv()
+        gh[...] = gr[oz, :, :] + gx[oz, :, :]
+        gz_copy(0).start()
+        gz_copy(1).start()
+        gx_copy(z).wait_recv()
+        m_ref[...] = gr[z, :, :] + gx[z, :, :]
+
     def fill_table(i, _):
         xx, yy, zz, _, _, _ = chip(lax.div(i, 2))
         d = dev(xx, yy, zz, lax.rem(i, 2))
@@ -370,54 +411,6 @@
     with jax.named_scope("table"):
         lax.fori_loop(0, 64, fill_table, 0)
 
-    def gx_copy(n):
-        return rcopy(gr.at[n], gx.at[n], gx_s + n, gx_r + n, peer_c)
-
-    with jax.named_scope("rows2wait"):
-        for zz in range(2):
-            gr[zz, :, :] = gram(r1[zz, v, :, :, :].reshape(4 * S_DEV, BLK))
-        gr[2, :, :] = gram(g1[...].reshape(4 * S_DEV, BLK))
-        for k in (1, 3, 2):
-            rows2_copy(k).wait_recv()
-            for zz in range(2):
-                gr[zz, :, :] += gram(r2[zz, k, :, :, :].reshape(4 * S_DEV, BLK))
-
-    @pl.when(c == 1)
-    def _():
-        gx_copy(oz).start()
-        gx_copy(z).start()
-
-    wait_got(zb.at[7:16], zb_r + 1)
-    lax.fori_loop(7, 16, zb_add, 0)
-    for n in range(2):
-        rs1_copy(1, DOWN[n]).start()
-        rs1_copy(3, UP[n]).start()
-
-    def gz_copy(n):
-        half = pl.ds(n * HALF, HALF)
-        return rcopy(gh.at[half], gz.at[half], gz_s + n, gz_r + n, peer_w if n else peer_z)
-
-    gz_all = rcopy(gh, gz, gz_s + 2, gz_r + 2, peer_z)
-
-    @pl.when(c == 0)
-    def _():
-        with jax.named_scope("gx"):
-            gx_copy(oz).wait_recv()
-        gh[...] = gr[oz, :, :] + gx[oz, :, :]
-        gz_copy(0).start()
-        gz_copy(1).start()
-        gx_copy(z).wait_recv()
-        m_ref[...] = gr[z, :, :] + gx[z, :, :]
-
-    with jax.named_scope("relay"):
-        for n in range(2):
-            for k in (1, 3):
-                rel_copy(k, n).wait_recv()
-                m = (UP if k == 1 else DOWN)[n]
-                p = pair_of(wrap(u + k), wrap(v + m))
-                buf[c, p, 0:SENT, :] = buf[c, p, 0:SENT, :] + rel[k // 2, n, :, :]
-                rs1_copy(k, m).start()
-
     with jax.named_scope("g2wait"):
         for k in (1, 3, 2):
             g2_copy(k).wait_recv()
@@ -435,6 +428,18 @@
         gz_all.start()
         m_ref[...] = gh[...]
 
+    def relay():
+        with jax.named_scope("relay"):
+            for n in range(2):
+                for k in (1, 3):
+                    rel_copy(k, n).wait_recv()
+                    m = (UP if k == 1 else DOWN)[n]
+                    p = pair_of(wrap(u + k), wrap(v + m))
+                    buf[c, p, 0:SENT, :] = buf[c, p, 0:SENT, :] + rel[k // 2, n, :, :]
+                    rs1_copy(k, m).start()
+
+    relay()
+
     def factor(scale):
         m_ref[...] = (m_ref[...] + gz[...]) * scale + DAMPING * eye(BLK)
 
@@ -447,9 +452,9 @@
         xx, yy, zz, dz, dx, dy = chip(n)
         return rcopy(isl.at[zz, xx * 4 + yy], ss.at[n], s_s, s_r, chip_dev(n))
 
-    def s_start(n, _):
-        s_copy(n).start()
-        return 0
+    def s_start():
+        for n in range(31, 0, -1):
+            s_copy(n).start()
 
     def rs2_copy(k, part):
         rows = pl.ds(MAIN, HALF) if part else pl.ds(0, MAIN)
@@ -473,19 +478,16 @@
     def t_copy(n):
         return rcopy(dd.at[n], tt.at[n], t_s, t_r, chip_dev(n))
 
-    def t_start(n, _):
-        t_copy(n).start()
-        return 0
-
     def slots_back():
         ss[0, :, :] = isl[z, x * 4 + y, :, :]
         with jax.named_scope("s"):
             wait_got(ss.at[1:32], s_r)
         with jax.named_scope("select"):
-            for n in range(32):
+            for n in range(31, -1, -1):
                 for cc in range(2):
                     dd[n, cc, :, :] = ss[table[2 * n + cc], :, :]
-            lax.fori_loop(1, 32, t_start, 0)
+                if n:
+                    t_copy(n).start()
         tt[0, :, :, :] = dd[0, :, :, :]
 
     @pl.when(c == 0)
@@ -503,23 +505,23 @@
             isx[zz, :, :, :] = x_ref[HALF:, cols].reshape(16, 8, HALF)
             isl[zz, :, :, :] = x_ref[:HALF, cols].reshape(16, 8, HALF)
         half_copy.start()
-        lax.fori_loop(1, 32, s_start, 0)
+        s_start()
         rs1_finish()
         slots_back()
 
     @pl.when(c == 1)
     def _():
-        with jax.named_scope("half"):
-            half_copy.wait_recv()
-        lax.fori_loop(1, 32, s_start, 0)
-        rs1_finish()
         core1_factor()
         with jax.named_scope("newton_begin"):
             newton_begin(m_ref, x_ref, e_ref)
-        slots_back()
+        with jax.named_scope("half"):
+            half_copy.wait_recv()
+        s_start()
+        rs1_finish()
         with jax.named_scope("newton_end"):
             newton_end(x_ref, e_ref)
         ginv_copy.start()
+        slots_back()
 
     with jax.named_scope("drain"):
         wait_sent(picks.at[:, 0:12], pick_s)
@@ -538,7 +540,7 @@
 
         @pl.when(c == 1)
         def _():
-            for copy in [gx_copy(oz), gx_copy(z), gz_all, ginv_copy]:
+            for copy in [gx_copy(oz), gx_copy(z), gz_all]:
                 copy.wait_send()
 
     with jax.named_scope("rs2a"):
@@ -605,6 +607,11 @@
         wait_sent(rs2b.at[1:4], rs2_s + 1)
         for copy in [rs3_copy, rs4_copy, out_copy]:
             copy.wait_send()
+
+        @pl.when(c == 1)
+        def _():
+            ginv_copy.wait_send()
+
     with jax.named_scope("store"):
         step_copy.wait()
         slot_copy.wait()

time: 62.8 us -> 62.6 us (level)
  no operation moved by 1% of the time
where the time goes in v4:
time: 62.6 us; the launch traced here: 62.5 us
  Pallas kernels  61.9 us (99%)
  between operations  0.64 us (1%)
    pallas_call x1, Pallas kernels, per_device(): pl.pallas_call(kernel, out_shape=(jax.ShapeDtypeStruct((HALF, BLK), F32),...  60.1 us
    pallas_call x1, Pallas kernels, per_device(): pl.pallas_call(settle, out_shape=(jax.ShapeDtypeStruct((HALF, BLK), F32),...  1.78 us

profile of v4, /device:TPU:1, one launch (start us, length us, event | category | flops | bytes accessed | tf_op | source)
XLA Modules:
  0.0 62.5 jit_solution(1957974339483667574)
XLA Ops:
  0.6 60.1 %shard_map.59 = (f32[128,256]{1,0:T(8,128)}, f32[2,128,256]{2,1,0:T(8,128)}) custom-call(bf16[768,8192]{1,0:T(8,128)(2,1)} %act_hbm.1, bf16[768,256]{1,0:T(8,128)(2,1)} %cot_hbm.1, s32[1,64]{1,0:T(1,128)} %bitcast.2, s32[32]{0:T(128)} %owner_ref.1), custom_call_target="tpu_custom_call" | custom-call | tf_op jit(solution)/shard_map/pallas_call | solution.py:628
  60.7 1.8 %shard_map.60 = (f32[128,256]{1,0:T(8,128)}, f32[2,128,256]{2,1,0:T(8,128)}) custom-call(f32[128,256]{1,0:T(8,128)} %get-tuple-element.6.step_in, f32[2,128,256]{2,1,0:T(8,128)} %get-tuple-element.7.slot_in), custom_call_target="tpu_custom_call" | custom-call | tf_op jit(solution)/shard_map/pallas_call | solution.py:692

commit v5 on v4

--- a/solution.py
+++ b/solution.py
@@ -518,9 +518,6 @@
             half_copy.wait_recv()
         s_start()
         rs1_finish()
-        with jax.named_scope("newton_end"):
-            newton_end(x_ref, e_ref)
-        ginv_copy.start()
         slots_back()
 
     with jax.named_scope("drain"):
@@ -548,6 +545,13 @@
     acc2[...] = acc1[0, 0:MAIN, :] + rs2a[1, :, :] + rs2a[2, :, :] + rs2a[3, :, :]
     rs3_copy = rcopy(acc2, rs3, rs3_s, rs3_r, peer_z)
     rs3_copy.start()
+
+    @pl.when(c == 1)
+    def _():
+        with jax.named_scope("newton_end"):
+            newton_end(x_ref, e_ref)
+        ginv_copy.start()
+
     with jax.named_scope("rs2b"):
         wait_got(rs2b.at[1:4], rs2_r + 1)
     fin[c, :, :] = acc1[0, MAIN:SENT, :] + rs2b[1, :, :] + rs2b[2, :, :] + rs2b[3, :, :]

time: 62.6 us -> 62.6 us (level)
  no operation moved by 1% of the time
where the time goes in v5:
time: 62.6 us; the launch traced here: 62.5 us
  Pallas kernels  61.9 us (99%)
  between operations  0.64 us (1%)
    pallas_call x1, Pallas kernels, per_device(): pl.pallas_call(kernel, out_shape=(jax.ShapeDtypeStruct((HALF, BLK), F32),...  60.1 us
    pallas_call x1, Pallas kernels, per_device(): pl.pallas_call(settle, out_shape=(jax.ShapeDtypeStruct((HALF, BLK), F32),...  1.78 us

profile of v5, /device:TPU:1, one launch (start us, length us, event | category | flops | bytes accessed | tf_op | source)
XLA Modules:
  0.0 62.5 jit_solution(11587837076887605123)
XLA Ops:
  0.6 60.1 %shard_map.59 = (f32[128,256]{1,0:T(8,128)}, f32[2,128,256]{2,1,0:T(8,128)}) custom-call(bf16[768,8192]{1,0:T(8,128)(2,1)} %act_hbm.1, bf16[768,256]{1,0:T(8,128)(2,1)} %cot_hbm.1, s32[1,64]{1,0:T(1,128)} %bitcast.2, s32[32]{0:T(128)} %owner_ref.1), custom_call_target="tpu_custom_call" | custom-call | tf_op jit(solution)/shard_map/pallas_call | solution.py:632
  60.7 1.8 %shard_map.60 = (f32[128,256]{1,0:T(8,128)}, f32[2,128,256]{2,1,0:T(8,128)}) custom-call(f32[128,256]{1,0:T(8,128)} %get-tuple-element.6.step_in, f32[2,128,256]{2,1,0:T(8,128)} %get-tuple-element.7.slot_in), custom_call_target="tpu_custom_call" | custom-call | tf_op jit(solution)/shard_map/pallas_call | solution.py:696
